TPU v7x, 256 devices: a whole 4x4x8 slice. The times are simulated.
256 devices in a mesh: leaf: 2 (over core), row: 4 (over x), col: 32 (over z, y).
Axes of the slice: x: 4, y: 4, z: 8, core: 2. Of those that a mesh axis runs over, the one named last changes fastest.
Arguments:
- child_rhs: float32 [512, 256, 256], P(('leaf', 'row', 'col')), may hold values from -6 to 6
- child_diag: float32 [512, 256, 256], P(('leaf', 'row', 'col')), may hold values from -0.375 to 0.375
- child_off: float32 [512, 256, 256], P(('leaf', 'row', 'col')), may hold values from -0.046875 to 0.046875
- live: int32 [512], P(('leaf', 'row', 'col')), may hold values from 1 to 256, 81920 in all
- targets: int32 [512, 256], P(('leaf', 'row', 'col')), may hold values from 0 to 2047
- top_rhs: float32 [2048, 256], P('row'), may hold values from -6 to 6
- top_factor: float32 [2048, 2048], P('row', 'col'), may hold values from -0.125 to 0.125
- top_diag: float32 [2048, 512], P('row'), may hold values from -0.25 to 0.25
Outputs:
- child_sol: float32 [512, 256, 256], P(('leaf', 'row', 'col'))
- top_sol: float32 [2048, 256], P('row')
All inputs are finite; a program needn't handle non-finite values. No bound on the sum of `live` on one device may be relied on, other than what follows from the above.
Results may differ from a plain program's by a relative error of at most 0.0003.
Values sent between devices are 32-bit elements; how exact they have to be, the bound alone decides.
A program may use at most 64 MiB of HBM per device.

v0:
```python
import jax
import jax.numpy as jnp
from jax import lax
from jax.sharding import PartitionSpec as P


def spread(value, axis, source):
    kept = jnp.where(lax.axis_index(axis) == source, value, 0).astype(value.dtype)
    return lax.psum(kept, axis)


def unit_lower(matrix):
    return jnp.tril(matrix) + jnp.eye(matrix.shape[-1], dtype=matrix.dtype)


def shards(child_rhs, child_diag, child_off, live, targets, top_rhs, top_factor, top_diag):
    highest = lax.Precision.HIGHEST
    owned_rows = top_rhs.shape[0]
    right_count = top_rhs.shape[1]
    block_size = top_diag.shape[1]
    owned_blocks = owned_rows // block_size
    row_count = lax.axis_size("row")
    top_order = owned_rows * row_count
    col_width = top_factor.shape[1]
    my_row = lax.axis_index("row")
    my_col = lax.axis_index("col")
    child_sol = jnp.einsum("bij,bjr->bir", unit_lower(child_diag), child_rhs, precision=highest)
    tiles = jnp.einsum("btj,bjr->btr", child_off, child_sol, precision=highest)
    slot_index = jnp.arange(child_off.shape[1], dtype=jnp.int32)
    keep = slot_index[None, :] < live[:, None]
    tiles = jnp.where(keep[:, :, None], tiles, jnp.zeros_like(tiles))
    contrib = jnp.zeros((top_order, right_count), jnp.float32)
    contrib = contrib.at[targets.reshape(-1)].add(tiles.reshape(-1, right_count))
    row_part = lax.psum_scatter(contrib, "row", scatter_dimension=0, tiled=True)
    share = lax.psum_scatter(row_part, ("leaf", "col"), scatter_dimension=0, tiled=True)
    updates = lax.all_gather(share, ("leaf", "col"), axis=0, tiled=True)
    reduced = top_rhs - updates
    inverse_all = unit_lower(top_diag.reshape(owned_blocks, block_size, block_size))
    col_global = my_col * col_width + jnp.arange(col_width, dtype=jnp.int32)

    def step(block, solution):
        local = block % owned_blocks
        owner = block // owned_blocks
        factor_rows = top_factor
        factor_rows = jnp.where(
            (col_global < block * block_size)[None, :], factor_rows, jnp.zeros_like(factor_rows)
        )
        columns = lax.dynamic_slice_in_dim(solution, my_col * col_width, col_width, 0)
        partial_value = jnp.dot(
            factor_rows, columns, precision=highest, preferred_element_type=jnp.float32
        )
        block_inverse = lax.dynamic_index_in_dim(inverse_all, local, 0, keepdims=False)
        before = lax.psum(partial_value, "col")
        solved = jnp.dot(
            block_inverse, reduced - before, precision=highest, preferred_element_type=jnp.float32
        )
        solved = spread(solved, "row", owner)
        return lax.dynamic_update_slice_in_dim(solution, solved, block * block_size, 0)

    solution = lax.fori_loop(
        0, row_count * owned_blocks, step, jnp.zeros((top_order, right_count), jnp.float32)
    )
    top_sol = lax.dynamic_slice_in_dim(solution, my_row * owned_rows, owned_rows, 0)
    return (child_sol, top_sol)


def solution(mesh):
    in_specs = (
        P(("leaf", "row", "col"), None, None),
        P(("leaf", "row", "col"), None, None),
        P(("leaf", "row", "col"), None, None),
        P(("leaf", "row", "col")),
        P(("leaf", "row", "col"), None),
        P("row", None),
        P("row", "col"),
        P("row", None),
    )
    out_specs = (P(("leaf", "row", "col"), None, None), P("row", None))
    return jax.shard_map(shards, mesh=mesh, in_specs=in_specs, out_specs=out_specs, check_vma=False)
```

profile of v0, /device:TPU:7, one launch (start us, length us, event | category | flops | bytes accessed | tf_op | source)
XLA Modules:
  0.0 1157.9 jit_solution(9631845340324377303)
XLA Ops:
  7.2 0.0 reduce-scatter.3.cloned.1.call-start
  7.3 0.8 iota_compare_fusion.4
  8.1 0.7 copy.18
  8.8 1.2 copy.10
  10.0 1.1 fusion.14
  11.1 0.7 convolution_select_fusion.1
  11.8 4.7 scatter_custom_fusion
  16.5 0.0 reduce-scatter.3.cloned.1.call-update
  16.6 0.0 reduce-scatter.5.cloned.1.call-start
  16.6 33.4 %reduce-scatter.3.cloned.1.call-done = f32[512,256]{1,0:T(8,128)} async-done(((f32[2048,256]{1,0:T(8,128)}), f32[512,256]{1,0:T(8,128)}) %reduce-scatter.3.cloned.1.call-update) | async-done | bytes 524304 | tf_op jit(solution)/shard_map/reduce_scatter | solution.py:34
  50.0 0.0 reduce-scatter.5.cloned.1.call-update
  50.1 0.1 add_bitcast_fusion
  50.2 139.9 %reduce-scatter.5.cloned.1.call-done = f32[8,256]{1,0:T(8,128)} async-done(((f32[512,256]{1,0:T(8,128)}), f32[8,256]{1,0:T(8,128)}) %reduce-scatter.5.cloned.1.call-update) | async-done | bytes 8208 | tf_op jit(solution)/shard_map/reduce_scatter | solution.py:35
  190.1 132.5 %all_gather.3 = f32[512,256]{1,0:T(8,128)S(1)} all-gather(f32[8,256]{1,0:T(8,128)} %reduce-scatter.5.cloned.1.call-done), channel_id=1, replica_groups=mesh['leaf'=2,'row'=4,'col'=32] {'leaf','col'}, dimensions={0}, use_global_device_ids=true | all-gather | bytes 532480 | tf_op jit(solution)/shard_map/all_gather | solution.py:36
  322.6 0.1 sub.17
  322.7 1.5 broadcast.60.clone
  324.2 825.0 %while.16 = (s32[]{:T(128)}, f32[2048,256]{1,0:T(8,128)}, f32[512,64]{0,1:T(8,128)S(1)}, s32[]{:T(128)}, f32[512,256]{1,0:T(8,128)S(1)}, /*index=5*/f32[1,512,51...) while((s32[]{:T(128)}, f32[2048,256]{1,0:T(8,128)}, ...), condition=%wide.region_6.7_spmd.clone, body=%wide.region_3.6_spmd.clone.sunk | while | flops 906526848 | bytes 11731889 | solution.py:60
  324.2 2.3 fusion.35
  326.5 0.0 all-reduce.3.cloned.1.call-update
  326.6 0.0 all-reduce.5.cloned.1.call-start
  326.6 156.8 %all-reduce.3.cloned.1.call-done = f32[512,256]{1,0:T(8,128)} async-done(((f32[512,256]{1,0:T(8,128)}), f32[512,256]{1,0:T(8,128)}) %all-reduce.3.cloned.1.call-update) | async-done | bytes 524304 | tf_op jit(solution)/shard_map/while/body/eval_jaxpr/psum | solution.py:53
  483.4 3.7 fusion.36
  487.1 0.0 all-reduce.5.cloned.1.call-update
  487.1 47.3 %all-reduce.5.cloned.1.call-done = f32[512,256]{0,1:T(8,128)} async-done(((f32[512,256]{0,1:T(8,128)}), f32[512,256]{0,1:T(8,128)}) %all-reduce.5.cloned.1.call-update) | async-done | bytes 524304 | tf_op jit(solution)/shard_map/while/body/eval_jaxpr/psum | solution.py:9
  534.5 1.2 copy.20
  535.7 0.8 constant_dynamic-update-slice_fusion.2
  536.5 2.3 fusion.35
  538.9 0.0 all-reduce.5.cloned.1.call-start
  538.9 148.4 %all-reduce.3.cloned.1.call-done = f32[512,256]{1,0:T(8,128)} async-done(((f32[512,256]{1,0:T(8,128)}), f32[512,256]{1,0:T(8,128)}) %all-reduce.3.cloned.1.call-update) | async-done | bytes 524304 | tf_op jit(solution)/shard_map/while/body/eval_jaxpr/psum | solution.py:53
  687.4 3.7 fusion.36
  691.1 47.3 %all-reduce.5.cloned.1.call-done = f32[512,256]{0,1:T(8,128)} async-done(((f32[512,256]{0,1:T(8,128)}), f32[512,256]{0,1:T(8,128)}) %all-reduce.5.cloned.1.call-update) | async-done | bytes 524304 | tf_op jit(solution)/shard_map/while/body/eval_jaxpr/psum | solution.py:9
  738.5 1.2 copy.20
  739.7 0.8 constant_dynamic-update-slice_fusion.2
  740.5 2.3 fusion.35
  742.9 0.0 all-reduce.5.cloned.1.call-start
  743.0 148.8 %all-reduce.3.cloned.1.call-done = f32[512,256]{1,0:T(8,128)} async-done(((f32[512,256]{1,0:T(8,128)}), f32[512,256]{1,0:T(8,128)}) %all-reduce.3.cloned.1.call-update) | async-done | bytes 524304 | tf_op jit(solution)/shard_map/while/body/eval_jaxpr/psum | solution.py:53
  891.7 3.7 fusion.36
  895.5 47.3 %all-reduce.5.cloned.1.call-done = f32[512,256]{0,1:T(8,128)} async-done(((f32[512,256]{0,1:T(8,128)}), f32[512,256]{0,1:T(8,128)}) %all-reduce.5.cloned.1.call-update) | async-done | bytes 524304 | tf_op jit(solution)/shard_map/while/body/eval_jaxpr/psum | solution.py:9
  942.8 1.2 copy.20
  944.0 0.8 constant_dynamic-update-slice_fusion.2
  944.9 2.3 fusion.35
  947.2 0.0 all-reduce.5.cloned.1.call-start
  947.3 148.8 %all-reduce.3.cloned.1.call-done = f32[512,256]{1,0:T(8,128)} async-done(((f32[512,256]{1,0:T(8,128)}), f32[512,256]{1,0:T(8,128)}) %all-reduce.3.cloned.1.call-update) | async-done | bytes 524304 | tf_op jit(solution)/shard_map/while/body/eval_jaxpr/psum | solution.py:53
  1096.0 3.7 fusion.36
  1099.8 47.3 %all-reduce.5.cloned.1.call-done = f32[512,256]{0,1:T(8,128)} async-done(((f32[512,256]{0,1:T(8,128)}), f32[512,256]{0,1:T(8,128)}) %all-reduce.5.cloned.1.call-update) | async-done | bytes 524304 | tf_op jit(solution)/shard_map/while/body/eval_jaxpr/psum | solution.py:9
  1147.1 1.2 copy.20
  1148.4 0.8 constant_dynamic-update-slice_fusion.2
  1149.2 1.9 constant_dynamic-slice_fusion
  (28 shorter events, 0.2 us)
Async XLA Ops:
  7.2 2.9 copy-start
  7.2 3.9 copy-start.5
  7.2 42.8 %reduce-scatter.3.cloned.1.call-start = ((), (), s32[]{:S(2)}) async-start(), calls=%async_computation.2 | async-start | bytes 2621440 | tf_op jit(solution)/shard_map/reduce_scatter | solution.py:34
  11.1 5.4 copy-start.2
  11.8 38.3 %copy-start.3 = (f32[512,512]{1,0:T(8,128)S(1)}, f32[512,512]{1,0:T(8,128)}, u32[]{:S(2)}) copy-start(f32[512,512]{1,0:T(8,128)} %param.17) | copy-start | bytes 3145732
  16.6 173.5 %reduce-scatter.5.cloned.1.call-start = ((), (), s32[]{:S(2)}) async-start(), calls=%async_computation.3 | async-start | bytes 532480 | tf_op jit(solution)/shard_map/reduce_scatter | solution.py:35
  16.6 306.0 %copy-start.4 = (f32[512,256]{1,0:T(8,128)S(1)}, f32[512,256]{1,0:T(8,128)}, u32[]{:S(2)}) copy-start(f32[512,256]{1,0:T(8,128)} %param.15) | copy-start | bytes 1572868
  50.2 274.0 %copy-start.1 = (f32[512,64]{0,1:T(8,128)S(1)}, f32[512,64]{0,1:T(8,128)}, u32[]{:S(2)}) copy-start(f32[512,64]{0,1:T(8,128)} %param.16) | copy-start | bytes 393220
  324.2 159.2 %all-reduce.3.cloned.1.call-start = ((), (), s32[]{:S(2)}) async-start(), calls=%async_computation.4 | async-start | bytes 1048576 | tf_op jit(solution)/shard_map/while/body/eval_jaxpr/psum | solution.py:53
  326.6 207.9 %all-reduce.5.cloned.1.call-start = ((), (), s32[]{:S(2)}) async-start(), calls=%async_computation.5 | async-start | bytes 1048576 | tf_op jit(solution)/shard_map/while/body/eval_jaxpr/psum | solution.py:9
  536.5 150.9 %all-reduce.3.cloned.1.call-start = ((), (), s32[]{:S(2)}) async-start(), calls=%async_computation.4 | async-start | bytes 1048576 | tf_op jit(solution)/shard_map/while/body/eval_jaxpr/psum | solution.py:53
  538.9 199.6 %all-reduce.5.cloned.1.call-start = ((), (), s32[]{:S(2)}) async-start(), calls=%async_computation.5 | async-start | bytes 1048576 | tf_op jit(solution)/shard_map/while/body/eval_jaxpr/psum | solution.py:9
  740.5 151.2 %all-reduce.3.cloned.1.call-start = ((), (), s32[]{:S(2)}) async-start(), calls=%async_computation.4 | async-start | bytes 1048576 | tf_op jit(solution)/shard_map/while/body/eval_jaxpr/psum | solution.py:53
  742.9 199.9 %all-reduce.5.cloned.1.call-start = ((), (), s32[]{:S(2)}) async-start(), calls=%async_computation.5 | async-start | bytes 1048576 | tf_op jit(solution)/shard_map/while/body/eval_jaxpr/psum | solution.py:9
  944.9 151.2 %all-reduce.3.cloned.1.call-start = ((), (), s32[]{:S(2)}) async-start(), calls=%async_computation.4 | async-start | bytes 1048576 | tf_op jit(solution)/shard_map/while/body/eval_jaxpr/psum | solution.py:53
  947.2 199.9 %all-reduce.5.cloned.1.call-start = ((), (), s32[]{:S(2)}) async-start(), calls=%async_computation.5 | async-start | bytes 1048576 | tf_op jit(solution)/shard_map/while/body/eval_jaxpr/psum | solution.py:9
Sparse Core Ops, SparseCore 0:
  16.7 33.3 reduce-scatter.2
  54.5 135.5 reduce-scatter.4
  329.4 153.9 all-reduce.2
  487.2 47.1 all-reduce.4
  541.4 145.9 all-reduce.2
  691.2 47.1 all-reduce.4
  745.7 145.9 all-reduce.2
  895.6 47.1 all-reduce.4
  950.1 145.9 all-reduce.2
  1099.9 47.1 all-reduce.4
where the time goes:
time: 1160 us
  waiting for transfers between devices  965 us (83%)
  blocking collectives  133 us (11%)
  matrix products  25.9 us (2%)
  between operations  14.2 us (1%)
  local copies, waits for them, and re-layouts  13.6 us (1%)
    psum x4, waiting for transfers between devices, step(): before = lax.psum(partial_value, 'col')  603 us
    psum x4, waiting for transfers between devices, spread(): return lax.psum(kept, axis)  189 us
    reduce_scatter x1, waiting for transfers between devices, shards(): lax.psum_scatter(row_part, ('leaf', 'col'), scatter_dimension=0, tiled=True)  140 us
    all_gather x1, blocking collectives, shards(): updates = lax.all_gather(share, ('leaf', 'col'), axis=0, tiled=True)  133 us
    reduce_scatter x1, waiting for transfers between devices, shards(): row_part = lax.psum_scatter(contrib, 'row', scatter_dimension=0, tiled=True)  33.4 us
  transfers between devices with their start and end apart: 10, of which 10 were waited for; matrix products, arithmetic and copies ran while one was open for 0% of the time, Pallas kernels for 0%

commit v1 on v0

v1 whole, which is shorter than its diff:
```python
import jax
import jax.numpy as jnp
from jax import lax
from jax.experimental import pallas as pl
from jax.experimental.pallas import tpu as pltpu
from jax.sharding import PartitionSpec as P

MESH = pl.DeviceIdType.MESH
F32 = jnp.float32
BF16 = jnp.bfloat16
NX, NY, NZ = 4, 4, 8


def split(value):
    high = value.astype(BF16)
    return high, (value - high.astype(F32)).astype(BF16)


def dot(a, b):
    return jnp.dot(a, b, preferred_element_type=F32)


def dot3(a, b):
    ah, al = split(a)
    bh, bl = split(b)
    return dot(ah, bh) + (dot(ah, bl) + dot(al, bh))


def tril(value, row0, col0):
    rows = lax.broadcasted_iota(jnp.int32, value.shape, 0) + row0
    cols = lax.broadcasted_iota(jnp.int32, value.shape, 1) + col0
    return jnp.where(rows >= cols, value, 0.0), rows == cols


def kernel(
    live_ref, targ_ref, rhs_hbm, diag_hbm, off_hbm, trhs_hbm, fac_hbm, td_hbm,
    csol_hbm, top_hbm,
    rhs_v, diag_v, off_v, csol_v, tile_v, trhs_v, fac_v, td_v,
    tg, trecv, tcol, tt, cbuf, s1recv, s2src, s2recv, s3src, s3recv,
    rhst, tinv, gsrc, grecv, fsrc, xrecv, f1recv, pbuf, outv,
    load_sem, out_sem, tgs, tgr, cs, cr, gs, gr, s1s, s1r, s2s, s2r, s3s, s3r, xs, xr, f1s, f1r, f2s, f2r,
):
    leaf, x, col = lax.axis_index("leaf"), lax.axis_index("row"), lax.axis_index("col")
    y, z = col % NY, col // NY
    sibling = 1 - leaf

    def local(src, dst, sem):
        return pltpu.make_async_copy(src, dst, sem)

    def remote(src, dst, send, recv, l2, x2, y2, z2):
        return pltpu.make_async_remote_copy(
            src_ref=src, dst_ref=dst, send_sem=send, recv_sem=recv,
            device_id=(l2, x2, z2 * NY + y2), device_id_type=MESH,
        )

    def arrived(ref, sem):
        pltpu.make_async_copy(ref, ref, sem).wait()

    loads = [
        local(diag_hbm, diag_v, load_sem.at[0]),
        local(rhs_hbm, rhs_v, load_sem.at[1]),
        local(off_hbm, off_v, load_sem.at[2]),
        local(td_hbm, td_v, load_sem.at[3]),
        local(fac_hbm, fac_v, load_sem.at[4]),
        local(trhs_hbm, trhs_v, load_sem.at[5]),
    ]
    for copy in loads:
        copy.start()

    barrier = pltpu.get_barrier_semaphore()
    mine = leaf * (NX * NY) + x * NY + y

    def greet_z(i, _):
        other = (mine + i) % (2 * NX * NY)
        l2, x2, y2 = other // (NX * NY), (other // NY) % NX, other % NY
        pl.semaphore_signal(barrier, inc=1, device_id=(l2, x2, z * NY + y2), device_id_type=MESH)
        return 0

    lax.fori_loop(1, 2 * NX * NY, greet_z, 0)

    def greet_x(i, _):
        z2 = (z + 1 + i // (2 * NY)) % NZ
        l2, y2 = (i // NY) % 2, i % NY
        pl.semaphore_signal(barrier, inc=1, device_id=(l2, x, z2 * NY + y2), device_id_type=MESH)
        return 0

    lax.fori_loop(0, (NZ - 1) * 2 * NY, greet_x, 0)

    lane = lax.broadcasted_iota(jnp.int32, (1, 256), 1)
    for s in range(2):
        row = jnp.where(lane < live_ref[s], targ_ref[s : s + 1, :], -1).astype(F32)
        tg[0, s, :, :] = jnp.broadcast_to(row, (8, 256))

    pl.semaphore_wait(barrier, 2 * NX * NY - 1 + (NZ - 1) * 2 * NY)

    tg_copy = remote(tg.at[0], tg.at[1], tgs, tgr, sibling, x, y, z)
    tg_copy.start()

    loads[0].wait()
    loads[1].wait()
    loads[2].wait()
    core_copies = []
    for s in range(2):
        low, _ = tril(diag_v[s], 0, 0)
        sol = rhs_v[s] + dot3(low, rhs_v[s])
        csol_v[s] = sol
        tile_v[s] = dot3(off_v[s], sol)
        copy = remote(
            tile_v.at[s, :, pl.ds(pl.multiple_of(sibling * 128, 128), 128)], trecv.at[s],
            cs.at[s], cr.at[s], sibling, x, y, z,
        )
        copy.start()
        core_copies.append(copy)
    csol_copy = local(csol_v, csol_hbm, out_sem.at[0])
    csol_copy.start()

    loads[3].wait()
    loads[4].wait()
    low, _ = tril(td_v[...], 0, 0)
    fac = fac_v[...]
    gt = (fac + dot3(low, fac)).T
    for y2 in range(NY):
        gsrc[y2] = gt[:, 128 * y2 : 128 * y2 + 128]

    def g_copy(i):
        y2 = (y + i % NY) % NY
        z2 = 2 * (i // NY) + leaf
        own = (y2 == y) & (z2 == z) & (z % 2 == leaf)
        return own, remote(
            gsrc.at[y2], grecv.at[z // 2, y], gs.at[i], gr.at[z // 2], z % 2, x, y2, z2
        ), local(gsrc.at[y2], grecv.at[z // 2, y], gr.at[z // 2])

    def g_start(i, _):
        own, there, here = g_copy(i)

        @pl.when(own)
        def _():
            here.start()

        @pl.when(jnp.logical_not(own))
        def _():
            there.start()

        return 0

    @pl.when(z // 2 < x)
    def _():
        lax.fori_loop(0, 16, g_start, 0)

    row0, col0 = pl.multiple_of(y * 128, 128), pl.multiple_of(leaf * 256, 256)
    low, eye = tril(td_v[pl.ds(row0, 128), pl.ds(col0, 256)], row0, col0)
    tinv[...] = (low + jnp.where(eye, 1.0, 0.0)).T
    loads[5].wait()
    rhst[...] = trhs_v[pl.ds(col0, 256), :].T

    half = pl.ds(pl.multiple_of(leaf * 128, 128), 128)
    for s in range(2):
        tcol[256 * s : 256 * s + 256, :] = jnp.broadcast_to(tg[0, s, 0:1, :], (128, 256)).T
        high, rest = split(tile_v[s, :, half].T)
        tt[0:128, 256 * s : 256 * s + 256] = high
        tt[128:256, 256 * s : 256 * s + 256] = rest
    tg_copy.wait_recv()
    for s in range(2):
        tcol[512 + 256 * s : 768 + 256 * s, :] = jnp.broadcast_to(tg[1, s, 0:1, :], (128, 256)).T
        core_copies[s].wait_recv()
        high, rest = split(trecv[s].T)
        tt[0:128, 512 + 256 * s : 768 + 256 * s] = high
        tt[128:256, 512 + 256 * s : 768 + 256 * s] = rest

    lane = lax.broadcasted_iota(jnp.int32, (1024, 128), 1)

    def contrib(q, d):
        block = (x + d) % NX
        rel = tcol[...] - (block * 512 + q * 256).astype(F32)
        lanes = lane.astype(F32)
        hot = jnp.concatenate(
            [jnp.where(rel == lanes, 1.0, 0.0), jnp.where(rel == lanes + 128.0, 1.0, 0.0)], axis=1
        ).astype(BF16)
        both = dot(tt[...], hot)
        cbuf[q, d] = both[0:128] + both[128:256]

    def s1_copy(q, d):
        return remote(
            cbuf.at[q, d], s1recv.at[q, d - 1], s1s.at[q, d], s1r.at[q], leaf, (x + d) % NX, y, z
        )

    for q in range(2):

        def s1_step(d, _, q=q):
            contrib(q, d)
            s1_copy(q, d).start()
            return 0

        lax.fori_loop(1, NX, s1_step, 0)
        contrib(q, 0)

    def s2_copy(q, e):
        z2 = (z + e) % NZ
        return remote(
            s2src.at[q, z2], s2recv.at[q, e - 1], s2s.at[q, e], s2r.at[q], leaf, x, y, z2
        )

    for q in range(2):
        arrived(s1recv.at[q], s1r.at[q])
        s2src[q] = (cbuf[q, 0] + s1recv[q, 0] + s1recv[q, 1] + s1recv[q, 2]).reshape(NZ, 16, 256)

        def s2_step(e, _, q=q):
            s2_copy(q, e).start()
            return 0

        lax.fori_loop(1, NZ, s2_step, 0)

    def s3_copy(q, dy):
        y2 = (y + dy) % NY
        return remote(s3src.at[q], s3recv.at[leaf, dy], s3s.at[q, dy], s3r, q, x, y2, z)

    for q in range(2):
        arrived(s2recv.at[q], s2r.at[q])
        total = s2src[q, z]
        for e in range(NZ - 1):
            total = total + s2recv[q, e]
        s3src[q] = total
        for dy in range(1, NY):
            s3_copy(q, dy).start()

        @pl.when(leaf == q)
        def _(q=q):
            local(s3src.at[q], s3recv.at[leaf, 0], s3r).start()

        @pl.when(leaf != q)
        def _(q=q):
            s3_copy(q, 0).start()

    arrived(s3recv, s3r)
    reds = []
    for h in range(2):
        upd = s3recv[h, 0] + s3recv[h, 1] + s3recv[h, 2] + s3recv[h, 3]
        reds.append(rhst[pl.ds(pl.multiple_of(h * 128 + z * 16, 16), 16), :] - upd)
    acc = dot3(jnp.concatenate(reds, axis=0), tinv[...])
    fsrc[...] = acc.reshape(2, 16, 128)

    def x_copy(k, x2, y2):
        return remote(
            fsrc, xrecv.at[k, leaf, y % 2], xs.at[x2, y2], xr.at[k], y // 2, x2, y2, z
        )

    for k in range(NX - 1):

        @pl.when(x == k)
        def _(k=k):
            for x2 in range(k + 1, NX):
                for y2 in range(NY):
                    x_copy(k, x2, y2).start()

        @pl.when(x > k)
        def _(k=k):
            arrived(grecv.at[k], gr.at[k])
            arrived(xrecv.at[k], xr.at[k])
            parts = (xrecv[k, 0] + xrecv[k, 1]).reshape(2, 32, 128)
            solved = jnp.concatenate([parts[0], parts[1]], axis=1)
            step = dot3(solved, grecv[k].reshape(256, 128))
            fsrc[...] = fsrc[...] - step.reshape(2, 16, 128)

    def f1_copy(h, e):
        z2 = (z + e) % NZ
        return remote(fsrc.at[h], f1recv.at[leaf, z], f1s.at[h, e], f1r, h, x, y, z2)

    for h in range(2):

        def f1_step(e, _, h=h):
            f1_copy(h, e).start()
            return 0

        lax.fori_loop(1, NZ, f1_step, 0)

        @pl.when(leaf == h)
        def _(h=h):
            local(fsrc.at[h], f1recv.at[leaf, z], f1r).start()

        @pl.when(leaf != h)
        def _(h=h):
            f1_copy(h, 0).start()

    arrived(f1recv, f1r)
    piece = (f1recv[0] + f1recv[1]).reshape(128, 128).T
    pbuf[...] = piece
    place = (pl.ds(row0, 128), half)

    def f2_copy(i):
        l2, y2 = (leaf + i // NY) % 2, (y + i % NY) % NY
        return remote(pbuf, outv.at[place[0], place[1]], f2s.at[i], f2r, l2, x, y2, z)

    def f2_step(i, _):
        f2_copy(i).start()
        return 0

    local(pbuf, outv.at[place[0], place[1]], f2r).start()
    lax.fori_loop(1, 2 * NY, f2_step, 0)
    arrived(outv, f2r)
    top_copy = local(outv, top_hbm, out_sem.at[1])
    top_copy.start()

    tg_copy.wait_send()
    for s in range(2):
        core_copies[s].wait_send()

    def g_wait(i, _):
        own, there, here = g_copy(i)

        @pl.when(jnp.logical_not(own))
        def _():
            there.wait_send()

        return 0

    @pl.when(z // 2 < x)
    def _():
        lax.fori_loop(0, 16, g_wait, 0)

    for q in range(2):
        for d in range(1, NX):
            s1_copy(q, d).wait_send()
        for e in range(1, NZ):
            s2_copy(q, e).wait_send()
        for dy in range(1, NY):
            s3_copy(q, dy).wait_send()

        @pl.when(leaf != q)
        def _(q=q):
            s3_copy(q, 0).wait_send()
            f1_copy(q, 0).wait_send()

        for e in range(1, NZ):
            f1_copy(q, e).wait_send()
    for k in range(NX - 1):

        @pl.when(x == k)
        def _(k=k):
            for x2 in range(k + 1, NX):
                for y2 in range(NY):
                    x_copy(k, x2, y2).wait_send()

    for i in range(1, 2 * NY):
        f2_copy(i).wait_send()
    csol_copy.wait()
    top_copy.wait()


def shards(child_rhs, child_diag, child_off, live, targets, top_rhs, top_factor, top_diag):
    any_ = pl.BlockSpec(memory_space=pl.ANY)
    vm = pltpu.VMEM
    dma = pltpu.SemaphoreType.DMA
    return pl.pallas_call(
        kernel,
        out_shape=(
            jax.ShapeDtypeStruct(child_rhs.shape, F32),
            jax.ShapeDtypeStruct(top_rhs.shape, F32),
        ),
        in_specs=[
            pl.BlockSpec(memory_space=pltpu.SMEM),
            pl.BlockSpec(memory_space=pltpu.VMEM),
        ] + [any_] * 6,
        out_specs=(any_, any_),
        scratch_shapes=[
            vm((2, 256, 256), F32), vm((2, 256, 256), F32), vm((2, 256, 256), F32),
            vm((2, 256, 256), F32), vm((2, 256, 256), F32),
            vm((512, 256), F32), vm((512, 64), F32), vm((512, 512), F32),
            vm((2, 2, 8, 256), F32), vm((2, 256, 128), F32), vm((1024, 128), F32), vm((256, 1024), BF16),
            vm((2, 4, 128, 256), F32), vm((2, 3, 128, 256), F32),
            vm((2, 8, 16, 256), F32), vm((2, 7, 16, 256), F32),
            vm((2, 16, 256), F32), vm((2, 4, 16, 256), F32),
            vm((256, 256), F32), vm((256, 128), F32),
            vm((4, 64, 128), F32), vm((3, 4, 64, 128), F32),
            vm((2, 16, 128), F32), vm((3, 2, 2, 2, 16, 128), F32),
            vm((2, 8, 16, 128), F32), vm((128, 128), F32), vm((512, 256), F32),
            dma((6,)), dma((2,)), dma, dma, dma((2,)), dma((2,)), dma((16,)), dma((4,)),
            dma((2, 4)), dma((2,)), dma((2, 8)), dma((2,)), dma((2, 4)), dma,
            dma((4, 4)), dma((3,)), dma((2, 8)), dma, dma((8,)), dma,
        ],
        compiler_params=pltpu.CompilerParams(collective_id=0, has_side_effects=True),
    )(live, targets, child_rhs, child_diag, child_off, top_rhs, top_factor, top_diag)


def solution(mesh):
    parts = ("leaf", "row", "col")
    in_specs = (
        P(parts, None, None),
        P(parts, None, None),
        P(parts, None, None),
        P(parts),
        P(parts, None),
        P("row", None),
        P("row", "col"),
        P("row", None),
    )
    out_specs = (P(parts, None, None), P("row", None))
    return jax.shard_map(shards, mesh=mesh, in_specs=in_specs, out_specs=out_specs, check_vma=False)
```

time: 1160 us -> 73.3 us (0.06)
  waiting for transfers between devices: 965 us -> 0 us
  blocking collectives: 133 us -> 0 us
  Pallas kernels: 0 us -> 68 us
  matrix products: 25.9 us -> 0 us
  between operations: 14.2 us -> 0.65 us
    psum x8 -> x0, waiting for transfers between devices: 792 us -> none  [the longest x4 603 us: step(): before = lax.psum(partial_value, 'col')]
    reduce_scatter x2 -> x0, waiting for transfers between devices: 173 us -> none  [the longest x1 140 us: shards(): lax.psum_scatter(row_part, ('leaf', 'col'), scatter_dimension=0, tiled=True)]
    all_gather x1 -> x0, blocking collectives: 133 us -> none  [shards(): updates = lax.all_gather(share, ('leaf', 'col'), axis=0, tiled=True)]
    pallas_call x0 -> x1, Pallas kernels: none -> 68 us  [shards(): pl.pallas_call(kernel, out_shape=(jax.ShapeDtypeStruct(child_rhs.shape, F...]
    dot_general x10 -> x0, matrix products: 25.9 us -> none  [the longest x4 14.8 us: step(): jnp.dot(block_inverse, reduced - before, precision=highest, preferred_ele...]
  transfers between devices with their start and end apart: 10 -> 0, of which waited for: 10 -> 0; matrix products, arithmetic and copies ran while one was open for 0% -> 0% of each run, Pallas kernels for 0% -> 0%
where the time goes in v1:
time: 73.3 us; the launch traced here: 73.2 us
  Pallas kernels  68 us (93%)
  local copies, waits for them, and re-layouts  4.46 us (6%)
    pallas_call x1, Pallas kernels, shards(): pl.pallas_call(kernel, out_shape=(jax.ShapeDtypeStruct(child_rhs.shape, F...  68 us
    unnamed x5, local copies, waits for them, and re-layouts  4.46 us

profile of v1, /device:TPU:7, one launch (start us, length us, event | category | flops | bytes accessed | tf_op | source)
XLA Modules:
  0.0 73.2 jit_solution(6887931205190351436)
XLA Ops:
  0.6 1.7 %copy.10.fac_hbm = f32[512,64]{1,0:T(8,128)} copy(f32[512,64]{0,1:T(8,128)} %param.14) | data formatting | bytes 262144 | tf_op args[6]
  2.4 68.0 %shard_map.95 = (f32[2,256,256]{2,1,0:T(8,128)}, f32[512,256]{1,0:T(8,128)}) custom-call(s32[2]{0:T(128)} %live_ref.1, s32[2,256]{1,0:T(2,128)} %targ_ref.1, f32[2,256,256]{2,1,0:T(8,128)} %rhs_hbm.1, f32[2,256,256]{2,1,0:T(8,128)} %diag_hbm.1, f32[2,256,256]{2,1,0:T(8,128)} %off_hbm.1, f32[512,256]{1,0:T(8,128)} %trhs_hbm.1, f32[512,64]{1,0:T(8,128)} %copy.10.fac_hbm, ...), custom_call_target="tpu_custom_call" | custom-call | tf_op jit(solution)/shard_map/pallas_call | solution.py:353
  70.4 0.0 copy-start
  70.4 1.9 %copy.13 = f32[2,256,256]{2,1,0:T(8,128)} copy(f32[2,256,256]{2,1,0:T(8,128)} %get-tuple-element.4) | data formatting | bytes 1048576
  72.4 0.0 copy-done
  72.4 0.8 %copy.14 = f32[512,256]{1,0:T(8,128)} copy(f32[512,256]{1,0:T(8,128)S(1)} %copy-done) | data formatting | bytes 1048576
Async XLA Ops:
  70.4 1.9 %copy-start = (f32[512,256]{1,0:T(8,128)S(1)}, f32[512,256]{1,0:T(8,128)}, u32[]{:S(2)}) copy-start(f32[512,256]{1,0:T(8,128)} %get-tuple-element.5) | copy-start | bytes 1572868

commit v2 on v1

v2 whole, which is shorter than its diff:
```python
import jax
import jax.numpy as jnp
from jax import lax
from jax.experimental import pallas as pl
from jax.experimental.pallas import tpu as pltpu
from jax.sharding import PartitionSpec as P

MESH = pl.DeviceIdType.MESH
F32 = jnp.float32
BF16 = jnp.bfloat16
NX, NY, NZ = 4, 4, 8


def split(value):
    high = value.astype(BF16)
    return high, (value - high.astype(F32)).astype(BF16)


def dot(a, b):
    return jnp.dot(a, b, preferred_element_type=F32)


def dot3(a, b):
    ah, al = split(a)
    bh, bl = split(b)
    return dot(ah, bh) + (dot(ah, bl) + dot(al, bh))


def dott(a, b):
    return lax.dot_general(a, b, (((1,), (1,)), ((), ())), preferred_element_type=F32)


def dot3t(a, b):
    ah, al = split(a)
    bh, bl = split(b)
    return dott(ah, bh) + (dott(ah, bl) + dott(al, bh))


def tril(value, row0, col0):
    rows = lax.broadcasted_iota(jnp.int32, value.shape, 0) + row0
    cols = lax.broadcasted_iota(jnp.int32, value.shape, 1) + col0
    return jnp.where(rows >= cols, value, 0.0), rows == cols


def kernel(
    live_ref, targ_ref, rhs_hbm, diag_hbm, off_hbm, trhs_hbm, fac_hbm, td_hbm,
    csol_v, outv,
    rhs_v, diag_v, off_v, tile_v, trhs_v, fac_v, td_v,
    tg, trecv, tcol, tt, cbuf, s1recv, s2src, s2recv, s3src, s3recv,
    rhst, tinv, gsrc, grecv, fsrc, xrecv, f1recv,
    load_sem, tgs, tgr, cs, cr, gas, gar, gs, gr, s1s, s1r, s2s, s2r, s3s, s3r, xs, xr, f1s, f1r, f2s, f2r, f3s, f3r,
):
    leaf, x, col = lax.axis_index("leaf"), lax.axis_index("row"), lax.axis_index("col")
    y, z = col % NY, col // NY
    sibling = 1 - leaf

    def local(src, dst, sem):
        return pltpu.make_async_copy(src, dst, sem)

    def remote(src, dst, send, recv, l2, x2, y2, z2):
        return pltpu.make_async_remote_copy(
            src_ref=src, dst_ref=dst, send_sem=send, recv_sem=recv,
            device_id=(l2, x2, z2 * NY + y2), device_id_type=MESH,
        )

    def arrived(ref, sem):
        pltpu.make_async_copy(ref, ref, sem).wait()

    drain = []

    def finish():
        for wait in drain:
            wait()

    loads = [
        local(ref.at[s], buf.at[s], load_sem.at[i, s])
        for s in range(2)
        for i, (ref, buf) in enumerate(((diag_hbm, diag_v), (rhs_hbm, rhs_v), (off_hbm, off_v)))
    ] + [
        local(td_hbm, td_v, load_sem.at[3, 0]),
        local(fac_hbm, fac_v, load_sem.at[4, 0]),
        local(trhs_hbm, trhs_v, load_sem.at[5, 0]),
    ]
    for copy in loads:
        copy.start()

    barrier = pltpu.get_barrier_semaphore()

    def greet(l2, x2, y2, z2):
        pl.semaphore_signal(barrier, inc=1, device_id=(l2, x2, z2 * NY + y2), device_id_type=MESH)

    greet(sibling, x, y, z)
    for d in range(1, NX):
        greet(leaf, (x + d) % NX, y, z)
    for d in range(1, NY):
        greet(leaf, x, (y + d) % NY, z)
    for d in range(1, NZ):
        greet(leaf, x, y, (z + d) % NZ)

    lane = lax.broadcasted_iota(jnp.int32, (1, 256), 1)
    for s in range(2):
        row = jnp.where(lane < live_ref[s], targ_ref[s : s + 1, :], -1).astype(F32)
        tg[0, s, :, :] = jnp.broadcast_to(row, (8, 256))

    for s in range(2):
        loads[3 * s].wait()
        loads[3 * s + 1].wait()
        low, _ = tril(diag_v[s], 0, 0)
        sol = rhs_v[s] + dot3(low, rhs_v[s])
        csol_v[s] = sol
        loads[3 * s + 2].wait()
        tile_v[s] = dot3(off_v[s], sol)

    pl.semaphore_wait(barrier, 1 + NX - 1 + NY - 1 + NZ - 1)
    tg_copy = remote(tg.at[0], tg.at[1], tgs, tgr, sibling, x, y, z)
    tg_copy.start()
    drain.append(tg_copy.wait_send)
    core_copies = []
    for s in range(2):
        copy = remote(
            tile_v.at[s, :, pl.ds(pl.multiple_of(sibling * 128, 128), 128)], trecv.at[s],
            cs.at[s], cr.at[s], sibling, x, y, z,
        )
        copy.start()
        core_copies.append(copy)
        drain.append(copy.wait_send)

    giver = (leaf == z % 2) & (z // 2 < x)
    for load in loads[6:]:
        load.wait()

    def ga_copy(d):
        y2 = (y + d) % NY
        return remote(gsrc.at[y2], grecv.at[z // 2, y], gas.at[d], gar, leaf, x, y2, z)

    @pl.when(giver)
    def _():
        low, _ = tril(td_v[...], 0, 0)
        fac = fac_v[...]
        gt = fac + dot3t(fac, low)
        for y2 in range(NY):
            gsrc[y2] = gt[:, 128 * y2 : 128 * y2 + 128]
        for d in range(1, NY):
            ga_copy(d).start()
        local(gsrc.at[y], grecv.at[z // 2, y], gar).start()

    def gb_copy(d):
        return remote(
            grecv.at[z // 2], grecv.at[z // 2], gs.at[d], gr.at[z // 2], leaf, x, y, (z + d) % NZ
        )

    def g_forward():
        @pl.when(giver)
        def _():
            arrived(grecv.at[z // 2], gar)
            for d in range(1, NZ):
                gb_copy(d).start()

    def g_drain():
        @pl.when(giver)
        def _():
            for d in range(1, NY):
                ga_copy(d).wait_send()
            for d in range(1, NZ):
                gb_copy(d).wait_send()

    drain.append(g_drain)

    row0, col0 = pl.multiple_of(y * 128, 128), pl.multiple_of(leaf * 256, 256)
    low, eye = tril(td_v[pl.ds(row0, 128), pl.ds(col0, 256)], row0, col0)
    tinv[...] = (low + jnp.where(eye, 1.0, 0.0)).T
    rhst[...] = trhs_v[pl.ds(col0, 256), :].T

    half = pl.ds(pl.multiple_of(leaf * 128, 128), 128)
    for s in range(2):
        tcol[256 * s : 256 * s + 256, :] = jnp.broadcast_to(tg[0, s, 0:1, :], (128, 256)).T
        high, rest = split(tile_v[s, :, half].T)
        tt[0:128, 256 * s : 256 * s + 256] = high
        tt[128:256, 256 * s : 256 * s + 256] = rest
    tg_copy.wait_recv()
    for s in range(2):
        tcol[512 + 256 * s : 768 + 256 * s, :] = jnp.broadcast_to(tg[1, s, 0:1, :], (128, 256)).T
        core_copies[s].wait_recv()
        high, rest = split(trecv[s].T)
        tt[0:128, 512 + 256 * s : 768 + 256 * s] = high
        tt[128:256, 512 + 256 * s : 768 + 256 * s] = rest
    lane = lax.broadcasted_iota(jnp.int32, (1024, 128), 1)

    def contrib(q, d):
        block = (x + d) % NX
        rel = tcol[...] - (block * 512 + q * 256).astype(F32)
        lanes = lane.astype(F32)
        hot = jnp.concatenate(
            [jnp.where(rel == lanes, 1.0, 0.0), jnp.where(rel == lanes + 128.0, 1.0, 0.0)], axis=1
        ).astype(BF16)
        both = dot(tt[...], hot)
        cbuf[q, d] = both[0:128] + both[128:256]

    def s1_copy(q, d):
        return remote(
            cbuf.at[q, d], s1recv.at[q, d - 1], s1s.at[q, d], s1r.at[q], leaf, (x + d) % NX, y, z
        )

    for q in range(2):

        def s1_step(d, _, q=q):
            contrib(q, d)
            s1_copy(q, d).start()
            return 0

        lax.fori_loop(1, NX, s1_step, 0)
        drain += [s1_copy(q, d).wait_send for d in range(1, NX)]
        contrib(q, 0)
        if q == 0:
            g_forward()

    def s2_copy(q, e):
        z2 = (z + e) % NZ
        return remote(
            s2src.at[q, z2], s2recv.at[q, e - 1], s2s.at[q, e], s2r.at[q], leaf, x, y, z2
        )

    for q in range(2):
        arrived(s1recv.at[q], s1r.at[q])
        s2src[q] = (cbuf[q, 0] + s1recv[q, 0] + s1recv[q, 1] + s1recv[q, 2]).reshape(NZ, 16, 256)

        def s2_step(e, _, q=q):
            s2_copy(q, e).start()
            return 0

        lax.fori_loop(1, NZ, s2_step, 0)
        drain += [s2_copy(q, e).wait_send for e in range(1, NZ)]

    def s3_copy(q, dy):
        y2 = (y + dy) % NY
        return remote(s3src.at[q], s3recv.at[leaf, dy], s3s.at[q, dy], s3r, q, x, y2, z)

    for q in range(2):
        arrived(s2recv.at[q], s2r.at[q])
        total = s2src[q, z]
        for e in range(NZ - 1):
            total = total + s2recv[q, e]
        s3src[q] = total
        for dy in range(1, NY):
            s3_copy(q, dy).start()

        @pl.when(leaf == q)
        def _(q=q):
            local(s3src.at[q], s3recv.at[leaf, 0], s3r).start()

        @pl.when(leaf != q)
        def _(q=q):
            s3_copy(q, 0).start()

        def s3_drain(q=q):
            for dy in range(1, NY):
                s3_copy(q, dy).wait_send()

            @pl.when(leaf != q)
            def _():
                s3_copy(q, 0).wait_send()

        drain.append(s3_drain)

    arrived(s3recv, s3r)
    reds = []
    for h in range(2):
        upd = s3recv[h, 0] + s3recv[h, 1] + s3recv[h, 2] + s3recv[h, 3]
        reds.append(rhst[pl.ds(pl.multiple_of(h * 128 + z * 16, 16), 16), :] - upd)
    acc = dot3(jnp.concatenate(reds, axis=0), tinv[...])
    fsrc[...] = acc.reshape(2, 16, 128)

    def x_copy(k, x2, y2):
        return remote(
            fsrc, xrecv.at[k, leaf, y % 2], xs.at[x2, y2], xr.at[k], y // 2, x2, y2, z
        )

    for k in range(NX - 1):

        @pl.when(x == k)
        def _(k=k):
            for x2 in range(k + 1, NX):
                for y2 in range(NY):
                    x_copy(k, x2, y2).start()

        @pl.when(x > k)
        def _(k=k):
            @pl.when(z != 2 * k + leaf)
            def _():
                arrived(grecv.at[k], gr.at[k])

            arrived(xrecv.at[k], xr.at[k])
            parts = (xrecv[k, 0] + xrecv[k, 1]).reshape(2, 32, 128)
            solved = jnp.concatenate([parts[0], parts[1]], axis=1)
            step = dot3(solved, grecv[k].reshape(256, 128))
            fsrc[...] = fsrc[...] - step.reshape(2, 16, 128)

        def x_drain(k=k):
            @pl.when(x == k)
            def _():
                for x2 in range(k + 1, NX):
                    for y2 in range(NY):
                        x_copy(k, x2, y2).wait_send()

        drain.append(x_drain)

    def f1_copy(h, e):
        z2 = (z + e) % NZ
        return remote(fsrc.at[h], f1recv.at[leaf, z], f1s.at[h, e], f1r, h, x, y, z2)

    for h in range(2):

        def f1_step(e, _, h=h):
            f1_copy(h, e).start()
            return 0

        lax.fori_loop(1, NZ, f1_step, 0)

        @pl.when(leaf == h)
        def _(h=h):
            local(fsrc.at[h], f1recv.at[leaf, z], f1r).start()

        @pl.when(leaf != h)
        def _(h=h):
            f1_copy(h, 0).start()

        def f1_drain(h=h):
            for e in range(1, NZ):
                f1_copy(h, e).wait_send()

            @pl.when(leaf != h)
            def _():
                f1_copy(h, 0).wait_send()

        drain.append(f1_drain)

    arrived(f1recv, f1r)
    piece = (f1recv[0] + f1recv[1]).reshape(128, 128).T
    def f2_part(d):
        return outv.at[pl.ds(pl.multiple_of((y + d) % NY * 128, 128), 128), half]

    def f2_copy(d):
        return remote(f2_part(0), f2_part(0), f2s.at[d], f2r.at[d], leaf, x, (y + d) % NY, z)

    def f3_copy(d):
        part = f2_part((NY - d) % NY)
        return remote(part, part, f3s.at[d], f3r, sibling, x, y, z)

    outv[pl.ds(row0, 128), half] = piece
    for d in range(1, NY):
        f2_copy(d).start()
    f3_copy(0).start()
    for d in range(1, NY):
        arrived(f2_part(NY - d), f2r.at[d])
        f3_copy(d).start()
    drain += [f2_copy(d).wait_send for d in range(1, NY)]
    drain += [f3_copy(d).wait_send for d in range(NY)]
    arrived(outv.at[:, pl.ds(pl.multiple_of(sibling * 128, 128), 128)], f3r)
    finish()


def shards(child_rhs, child_diag, child_off, live, targets, top_rhs, top_factor, top_diag):
    any_ = pl.BlockSpec(memory_space=pl.ANY)
    vm = pltpu.VMEM
    dma = pltpu.SemaphoreType.DMA
    return pl.pallas_call(
        kernel,
        out_shape=(
            pltpu.VMEM(child_rhs.shape, F32),
            pltpu.VMEM(top_rhs.shape, F32),
        ),
        in_specs=[
            pl.BlockSpec(memory_space=pltpu.SMEM),
            pl.BlockSpec(memory_space=pltpu.VMEM),
        ] + [any_] * 6,
        out_specs=(pl.BlockSpec(memory_space=pltpu.VMEM),) * 2,
        scratch_shapes=[
            vm((2, 256, 256), F32), vm((2, 256, 256), F32), vm((2, 256, 256), F32),
            vm((2, 256, 256), F32),
            vm((512, 256), F32), vm((64, 512), F32), vm((512, 512), F32),
            vm((2, 2, 8, 256), F32), vm((2, 256, 128), F32), vm((1024, 128), F32), vm((256, 1024), BF16),
            vm((2, 4, 128, 256), F32), vm((2, 3, 128, 256), F32),
            vm((2, 8, 16, 256), F32), vm((2, 7, 16, 256), F32),
            vm((2, 16, 256), F32), vm((2, 4, 16, 256), F32),
            vm((256, 256), F32), vm((256, 128), F32),
            vm((4, 64, 128), F32), vm((3, 4, 64, 128), F32),
            vm((2, 16, 128), F32), vm((3, 2, 2, 2, 16, 128), F32),
            vm((2, 8, 16, 128), F32),
            dma((6, 2)), dma, dma, dma((2,)), dma((2,)), dma((4,)), dma, dma((8,)), dma((4,)),
            dma((2, 4)), dma((2,)), dma((2, 8)), dma((2,)), dma((2, 4)), dma,
            dma((4, 4)), dma((3,)), dma((2, 8)), dma, dma((4,)), dma((4,)), dma((4,)), dma,
        ],
        compiler_params=pltpu.CompilerParams(collective_id=0, has_side_effects=True),
    )(live, targets, child_rhs, child_diag, child_off, top_rhs, top_factor.T, top_diag)


def solution(mesh):
    parts = ("leaf", "row", "col")
    in_specs = (
        P(parts, None, None),
        P(parts, None, None),
        P(parts, None, None),
        P(parts),
        P(parts, None),
        P("row", None),
        P("row", "col"),
        P("row", None),
    )
    out_specs = (P(parts, None, None), P("row", None))
    return jax.shard_map(shards, mesh=mesh, in_specs=in_specs, out_specs=out_specs, check_vma=False)
```

time: 73.3 us -> 63.8 us (0.87)
  Pallas kernels: 68 us -> 61.5 us
  local copies, waits for them, and re-layouts: 4.46 us -> 1.59 us
    pallas_call x1, Pallas kernels: 68 us -> 61.5 us  [shards(): pl.pallas_call(kernel, out_shape=(pltpu.VMEM(child_rhs.shape, F32), pltpu...]
    unnamed x5 -> x2, local copies, waits for them, and re-layouts: 4.46 us -> 1.59 us
where the time goes in v2:
time: 63.8 us; the launch traced here: 63.7 us
  Pallas kernels  61.5 us (96%)
  local copies, waits for them, and re-layouts  1.59 us (2%)
  between operations  0.64 us (1%)
    pallas_call x1, Pallas kernels, shards(): pl.pallas_call(kernel, out_shape=(pltpu.VMEM(child_rhs.shape, F32), pltpu...  61.5 us
    unnamed x2, local copies, waits for them, and re-layouts  1.59 us

profile of v2, /device:TPU:7, one launch (start us, length us, event | category | flops | bytes accessed | tf_op | source)
XLA Modules:
  0.0 63.7 jit_solution(16121859545519126458)
XLA Ops:
  0.6 61.5 %shard_map.95 = (f32[2,256,256]{2,1,0:T(8,128)S(1)}, f32[512,256]{1,0:T(8,128)S(1)}) custom-call(s32[2]{0:T(128)} %live_ref.1, s32[2,256]{1,0:T(2,128)} %targ_ref.1, f32[2,256,256]{2,1,0:T(8,128)} %rhs_hbm.1, f32[2,256,256]{2,1,0:T(8,128)} %diag_hbm.1, f32[2,256,256]{2,1,0:T(8,128)} %off_hbm.1, f32[512,256]{1,0:T(8,128)} %trhs_hbm.1, f32[64,512]{1,0:T(8,128)} %bitcast.1, ...), custom_call_target="tpu_custom_call" | custom-call | tf_op jit(solution)/shard_map/pallas_call | solution.py:366
  62.1 0.8 %copy.12 = f32[2,256,256]{2,1,0:T(8,128)} copy(f32[2,256,256]{2,1,0:T(8,128)S(1)} %get-tuple-element.2) | data formatting | bytes 1048576
  62.9 0.8 %copy.13 = f32[512,256]{1,0:T(8,128)} copy(f32[512,256]{1,0:T(8,128)S(1)} %get-tuple-element.3) | data formatting | bytes 1048576

commit v3 on v2

--- a/solution.py
+++ b/solution.py
@@ -26,6 +26,13 @@
     return dot(ah, bh) + (dot(ah, bl) + dot(al, bh))
 
 
+def dot3p(a, bh, bl):
+    n = a.shape[0]
+    ah, al = split(a)
+    both = dot(jnp.concatenate([ah, al], axis=0), bh)
+    return both[:n] + (dot(ah, bl) + both[n:])
+
+
 def dott(a, b):
     return lax.dot_general(a, b, (((1,), (1,)), ((), ())), preferred_element_type=F32)
 
@@ -47,8 +54,8 @@
     csol_v, outv,
     rhs_v, diag_v, off_v, tile_v, trhs_v, fac_v, td_v,
     tg, trecv, tcol, tt, cbuf, s1recv, s2src, s2recv, s3src, s3recv,
-    rhst, tinv, gsrc, grecv, fsrc, xrecv, f1recv,
-    load_sem, tgs, tgr, cs, cr, gas, gar, gs, gr, s1s, s1r, s2s, s2r, s3s, s3r, xs, xr, f1s, f1r, f2s, f2r, f3s, f3r,
+    rhst, tinv, gsrc, grecv, gparts, fsrc, xrecv, frecv, fown, fall,
+    load_sem, tgs, tgr, cs, cr, gas, gar, gs, gr, s1s, s1r, s2s, s2r, s3s, s3r, xs, xr, fps, fpr, f1s, f1r, f3s, f3r,
 ):
     leaf, x, col = lax.axis_index("leaf"), lax.axis_index("row"), lax.axis_index("col")
     y, z = col % NY, col // NY
@@ -168,7 +175,7 @@
 
     row0, col0 = pl.multiple_of(y * 128, 128), pl.multiple_of(leaf * 256, 256)
     low, eye = tril(td_v[pl.ds(row0, 128), pl.ds(col0, 256)], row0, col0)
-    tinv[...] = (low + jnp.where(eye, 1.0, 0.0)).T
+    tinv[0], tinv[1] = split((low + jnp.where(eye, 1.0, 0.0)).T)
     rhst[...] = trhs_v[pl.ds(col0, 256), :].T
 
     half = pl.ds(pl.multiple_of(leaf * 128, 128), 128)
@@ -262,12 +269,24 @@
 
         drain.append(s3_drain)
 
+    for k in range(NX - 1):
+
+        @pl.when(x > k)
+        def _(k=k):
+            @pl.when(z != 2 * k + leaf)
+            def _():
+                arrived(grecv.at[k], gr.at[k])
+
+            high, rest = split(grecv[k].reshape(256, 128))
+            gparts[k, 0] = high
+            gparts[k, 1] = rest
+
     arrived(s3recv, s3r)
     reds = []
     for h in range(2):
         upd = s3recv[h, 0] + s3recv[h, 1] + s3recv[h, 2] + s3recv[h, 3]
         reds.append(rhst[pl.ds(pl.multiple_of(h * 128 + z * 16, 16), 16), :] - upd)
-    acc = dot3(jnp.concatenate(reds, axis=0), tinv[...])
+    acc = dot3p(jnp.concatenate(reds, axis=0), tinv[0], tinv[1])
     fsrc[...] = acc.reshape(2, 16, 128)
 
     def x_copy(k, x2, y2):
@@ -285,14 +304,10 @@
 
         @pl.when(x > k)
         def _(k=k):
-            @pl.when(z != 2 * k + leaf)
-            def _():
-                arrived(grecv.at[k], gr.at[k])
-
             arrived(xrecv.at[k], xr.at[k])
             parts = (xrecv[k, 0] + xrecv[k, 1]).reshape(2, 32, 128)
             solved = jnp.concatenate([parts[0], parts[1]], axis=1)
-            step = dot3(solved, grecv[k].reshape(256, 128))
+            step = dot3p(solved, gparts[k, 0], gparts[k, 1])
             fsrc[...] = fsrc[...] - step.reshape(2, 16, 128)
 
         def x_drain(k=k):
@@ -304,57 +319,34 @@
 
         drain.append(x_drain)
 
-    def f1_copy(h, e):
-        z2 = (z + e) % NZ
-        return remote(fsrc.at[h], f1recv.at[leaf, z], f1s.at[h, e], f1r, h, x, y, z2)
-
-    for h in range(2):
-
-        def f1_step(e, _, h=h):
-            f1_copy(h, e).start()
-            return 0
-
-        lax.fori_loop(1, NZ, f1_step, 0)
-
-        @pl.when(leaf == h)
-        def _(h=h):
-            local(fsrc.at[h], f1recv.at[leaf, z], f1r).start()
-
-        @pl.when(leaf != h)
-        def _(h=h):
-            f1_copy(h, 0).start()
-
-        def f1_drain(h=h):
-            for e in range(1, NZ):
-                f1_copy(h, e).wait_send()
-
-            @pl.when(leaf != h)
-            def _():
-                f1_copy(h, 0).wait_send()
-
-        drain.append(f1_drain)
-
-    arrived(f1recv, f1r)
-    piece = (f1recv[0] + f1recv[1]).reshape(128, 128).T
-    def f2_part(d):
-        return outv.at[pl.ds(pl.multiple_of((y + d) % NY * 128, 128), 128), half]
-
-    def f2_copy(d):
-        return remote(f2_part(0), f2_part(0), f2s.at[d], f2r.at[d], leaf, x, (y + d) % NY, z)
-
-    def f3_copy(d):
-        part = f2_part((NY - d) % NY)
-        return remote(part, part, f3s.at[d], f3r, sibling, x, y, z)
-
-    outv[pl.ds(row0, 128), half] = piece
-    for d in range(1, NY):
-        f2_copy(d).start()
-    f3_copy(0).start()
-    for d in range(1, NY):
-        arrived(f2_part(NY - d), f2r.at[d])
-        f3_copy(d).start()
-    drain += [f2_copy(d).wait_send for d in range(1, NY)]
-    drain += [f3_copy(d).wait_send for d in range(NY)]
+    pair = remote(fsrc.at[sibling], frecv, fps, fpr, sibling, x, y, z)
+    pair.start()
+    drain.append(pair.wait_send)
+    pair.wait_recv()
+    fown[...] = fsrc[leaf] + frecv[...]
+
+    def f1_copy(dy, dz):
+        return remote(
+            fown, fall.at[y, z], f1s.at[dy, dz], f1r.at[y], leaf, x, (y + dy) % NY, (z + dz) % NZ
+        )
+
+    for dz in (4, 3, 5, 2, 6, 1, 7, 0):
+        for dy in (2, 1, 3, 0):
+            if dy or dz:
+                f1_copy(dy, dz).start()
+                drain.append(f1_copy(dy, dz).wait_send)
+    local(fown, fall.at[y, z], f1r.at[y]).start()
+
+    def f3_copy(y2):
+        part = outv.at[pl.ds(pl.multiple_of(y2 * 128, 128), 128), half]
+        return remote(part, part, f3s.at[y2], f3r, sibling, x, y, z)
+
+    for d in (0, 1, 3, 2):
+        y2 = (y + d) % NY
+        arrived(fall.at[y2], f1r.at[y2])
+        outv[pl.ds(pl.multiple_of(y2 * 128, 128), 128), half] = fall[y2].reshape(128, 128).T
+        f3_copy(y2).start()
+    drain += [f3_copy(y2).wait_send for y2 in range(NY)]
     arrived(outv.at[:, pl.ds(pl.multiple_of(sibling * 128, 128), 128)], f3r)
     finish()
 
@@ -382,13 +374,13 @@
             vm((2, 4, 128, 256), F32), vm((2, 3, 128, 256), F32),
             vm((2, 8, 16, 256), F32), vm((2, 7, 16, 256), F32),
             vm((2, 16, 256), F32), vm((2, 4, 16, 256), F32),
-            vm((256, 256), F32), vm((256, 128), F32),
-            vm((4, 64, 128), F32), vm((3, 4, 64, 128), F32),
+            vm((256, 256), F32), vm((2, 256, 128), BF16),
+            vm((4, 64, 128), F32), vm((3, 4, 64, 128), F32), vm((3, 2, 256, 128), BF16),
             vm((2, 16, 128), F32), vm((3, 2, 2, 2, 16, 128), F32),
-            vm((2, 8, 16, 128), F32),
+            vm((16, 128), F32), vm((16, 128), F32), vm((4, 8, 16, 128), F32),
             dma((6, 2)), dma, dma, dma((2,)), dma((2,)), dma((4,)), dma, dma((8,)), dma((4,)),
             dma((2, 4)), dma((2,)), dma((2, 8)), dma((2,)), dma((2, 4)), dma,
-            dma((4, 4)), dma((3,)), dma((2, 8)), dma, dma((4,)), dma((4,)), dma((4,)), dma,
+            dma((4, 4)), dma((3,)), dma, dma, dma((4, 8)), dma((4,)), dma((4,)), dma,
         ],
         compiler_params=pltpu.CompilerParams(collective_id=0, has_side_effects=True),
     )(live, targets, child_rhs, child_diag, child_off, top_rhs, top_factor.T, top_diag)

time: 63.8 us -> 61.8 us (0.969)
  Pallas kernels: 61.5 us -> 59.5 us
    pallas_call x1, Pallas kernels: 61.5 us -> 59.5 us  [shards(): pl.pallas_call(kernel, out_shape=(pltpu.VMEM(child_rhs.shape, F32), pltpu...]
where the time goes in v3:
time: 61.8 us; the launch traced here: 61.7 us
  Pallas kernels  59.5 us (96%)
  local copies, waits for them, and re-layouts  1.59 us (3%)
  between operations  0.64 us (1%)
    pallas_call x1, Pallas kernels, shards(): pl.pallas_call(kernel, out_shape=(pltpu.VMEM(child_rhs.shape, F32), pltpu...  59.5 us
    unnamed x2, local copies, waits for them, and re-layouts  1.59 us

profile of v3, /device:TPU:7, one launch (start us, length us, event | category | flops | bytes accessed | tf_op | source)
XLA Modules:
  0.0 61.7 jit_solution(3887079204879660088)
XLA Ops:
  0.6 59.5 %shard_map.95 = (f32[2,256,256]{2,1,0:T(8,128)S(1)}, f32[512,256]{1,0:T(8,128)S(1)}) custom-call(s32[2]{0:T(128)} %live_ref.1, s32[2,256]{1,0:T(2,128)} %targ_ref.1, f32[2,256,256]{2,1,0:T(8,128)} %rhs_hbm.1, f32[2,256,256]{2,1,0:T(8,128)} %diag_hbm.1, f32[2,256,256]{2,1,0:T(8,128)} %off_hbm.1, f32[512,256]{1,0:T(8,128)} %trhs_hbm.1, f32[64,512]{1,0:T(8,128)} %bitcast.1, ...), custom_call_target="tpu_custom_call" | custom-call | tf_op jit(solution)/shard_map/pallas_call | solution.py:358
  60.1 0.8 %copy.12 = f32[2,256,256]{2,1,0:T(8,128)} copy(f32[2,256,256]{2,1,0:T(8,128)S(1)} %get-tuple-element.2) | data formatting | bytes 1048576
  60.9 0.8 %copy.13 = f32[512,256]{1,0:T(8,128)} copy(f32[512,256]{1,0:T(8,128)S(1)} %get-tuple-element.3) | data formatting | bytes 1048576

commit v4 on v3

--- a/solution.py
+++ b/solution.py
@@ -55,7 +55,7 @@
     rhs_v, diag_v, off_v, tile_v, trhs_v, fac_v, td_v,
     tg, trecv, tcol, tt, cbuf, s1recv, s2src, s2recv, s3src, s3recv,
     rhst, tinv, gsrc, grecv, gparts, fsrc, xrecv, frecv, fown, fall,
-    load_sem, tgs, tgr, cs, cr, gas, gar, gs, gr, s1s, s1r, s2s, s2r, s3s, s3r, xs, xr, fps, fpr, f1s, f1r, f3s, f3r,
+    load_sem, tgs, tgr, cs, cr, gas, gar, gs, gr, s1s, s1r, s2s, s2r, s3s, s3r, xs, xr, fps, fpr, f1s, f1r, f2s, f2r, f3s, f3r,
 ):
     leaf, x, col = lax.axis_index("leaf"), lax.axis_index("row"), lax.axis_index("col")
     y, z = col % NY, col // NY
@@ -131,52 +131,6 @@
         copy.start()
         core_copies.append(copy)
         drain.append(copy.wait_send)
-
-    giver = (leaf == z % 2) & (z // 2 < x)
-    for load in loads[6:]:
-        load.wait()
-
-    def ga_copy(d):
-        y2 = (y + d) % NY
-        return remote(gsrc.at[y2], grecv.at[z // 2, y], gas.at[d], gar, leaf, x, y2, z)
-
-    @pl.when(giver)
-    def _():
-        low, _ = tril(td_v[...], 0, 0)
-        fac = fac_v[...]
-        gt = fac + dot3t(fac, low)
-        for y2 in range(NY):
-            gsrc[y2] = gt[:, 128 * y2 : 128 * y2 + 128]
-        for d in range(1, NY):
-            ga_copy(d).start()
-        local(gsrc.at[y], grecv.at[z // 2, y], gar).start()
-
-    def gb_copy(d):
-        return remote(
-            grecv.at[z // 2], grecv.at[z // 2], gs.at[d], gr.at[z // 2], leaf, x, y, (z + d) % NZ
-        )
-
-    def g_forward():
-        @pl.when(giver)
-        def _():
-            arrived(grecv.at[z // 2], gar)
-            for d in range(1, NZ):
-                gb_copy(d).start()
-
-    def g_drain():
-        @pl.when(giver)
-        def _():
-            for d in range(1, NY):
-                ga_copy(d).wait_send()
-            for d in range(1, NZ):
-                gb_copy(d).wait_send()
-
-    drain.append(g_drain)
-
-    row0, col0 = pl.multiple_of(y * 128, 128), pl.multiple_of(leaf * 256, 256)
-    low, eye = tril(td_v[pl.ds(row0, 128), pl.ds(col0, 256)], row0, col0)
-    tinv[0], tinv[1] = split((low + jnp.where(eye, 1.0, 0.0)).T)
-    rhst[...] = trhs_v[pl.ds(col0, 256), :].T
 
     half = pl.ds(pl.multiple_of(leaf * 128, 128), 128)
     for s in range(2):
@@ -217,9 +171,55 @@
 
         lax.fori_loop(1, NX, s1_step, 0)
         drain += [s1_copy(q, d).wait_send for d in range(1, NX)]
+
+    giver = (leaf == z % 2) & (z // 2 < x)
+    for load in loads[6:]:
+        load.wait()
+
+    def ga_copy(d):
+        y2 = (y + d) % NY
+        return remote(gsrc.at[y2], grecv.at[z // 2, y], gas.at[d], gar, leaf, x, y2, z)
+
+    @pl.when(giver)
+    def _():
+        low, _ = tril(td_v[...], 0, 0)
+        fac = fac_v[...]
+        gt = fac + dot3t(fac, low)
+        for y2 in range(NY):
+            gsrc[y2] = gt[:, 128 * y2 : 128 * y2 + 128]
+        for d in range(1, NY):
+            ga_copy(d).start()
+        local(gsrc.at[y], grecv.at[z // 2, y], gar).start()
+
+    def gb_copy(d):
+        return remote(
+            grecv.at[z // 2], grecv.at[z // 2], gs.at[d], gr.at[z // 2], leaf, x, y, (z + d) % NZ
+        )
+
+    def g_forward():
+        @pl.when(giver)
+        def _():
+            arrived(grecv.at[z // 2], gar)
+            for d in range(1, NZ):
+                gb_copy(d).start()
+
+    def g_drain():
+        @pl.when(giver)
+        def _():
+            for d in range(1, NY):
+                ga_copy(d).wait_send()
+            for d in range(1, NZ):
+                gb_copy(d).wait_send()
+
+    drain.append(g_drain)
+
+    row0, col0 = pl.multiple_of(y * 128, 128), pl.multiple_of(leaf * 256, 256)
+    low, eye = tril(td_v[pl.ds(row0, 128), pl.ds(col0, 256)], row0, col0)
+    tinv[0], tinv[1] = split((low + jnp.where(eye, 1.0, 0.0)).T)
+    rhst[...] = trhs_v[pl.ds(col0, 256), :].T
+
+    for q in range(2):
         contrib(q, 0)
-        if q == 0:
-            g_forward()
 
     def s2_copy(q, e):
         z2 = (z + e) % NZ
@@ -237,6 +237,7 @@
 
         lax.fori_loop(1, NZ, s2_step, 0)
         drain += [s2_copy(q, e).wait_send for e in range(1, NZ)]
+    g_forward()
 
     def s3_copy(q, dy):
         y2 = (y + dy) % NY
@@ -269,18 +270,6 @@
 
         drain.append(s3_drain)
 
-    for k in range(NX - 1):
-
-        @pl.when(x > k)
-        def _(k=k):
-            @pl.when(z != 2 * k + leaf)
-            def _():
-                arrived(grecv.at[k], gr.at[k])
-
-            high, rest = split(grecv[k].reshape(256, 128))
-            gparts[k, 0] = high
-            gparts[k, 1] = rest
-
     arrived(s3recv, s3r)
     reds = []
     for h in range(2):
@@ -304,6 +293,13 @@
 
         @pl.when(x > k)
         def _(k=k):
+            @pl.when(z != 2 * k + leaf)
+            def _():
+                arrived(grecv.at[k], gr.at[k])
+
+            high, rest = split(grecv[k].reshape(256, 128))
+            gparts[k, 0] = high
+            gparts[k, 1] = rest
             arrived(xrecv.at[k], xr.at[k])
             parts = (xrecv[k, 0] + xrecv[k, 1]).reshape(2, 32, 128)
             solved = jnp.concatenate([parts[0], parts[1]], axis=1)
@@ -325,17 +321,23 @@
     pair.wait_recv()
     fown[...] = fsrc[leaf] + frecv[...]
 
-    def f1_copy(dy, dz):
-        return remote(
-            fown, fall.at[y, z], f1s.at[dy, dz], f1r.at[y], leaf, x, (y + dy) % NY, (z + dz) % NZ
-        )
-
-    for dz in (4, 3, 5, 2, 6, 1, 7, 0):
-        for dy in (2, 1, 3, 0):
-            if dy or dz:
-                f1_copy(dy, dz).start()
-                drain.append(f1_copy(dy, dz).wait_send)
-    local(fown, fall.at[y, z], f1r.at[y]).start()
+    def f1_copy(d):
+        return remote(fown, fall.at[y, z], f1s.at[d], f1r.at[d], leaf, x, y, (z + d) % NZ)
+
+    def f2_copy(d, dy):
+        part = fall.at[y, (z + NZ - d) % NZ]
+        return remote(part, part, f2s.at[d, dy], f2r.at[y], leaf, x, (y + dy) % NY, z)
+
+    for d in (4, 3, 5, 2, 6, 1, 7):
+        f1_copy(d).start()
+        drain.append(f1_copy(d).wait_send)
+    fall[y, z] = fown[...]
+    for d in (0, 1, 7, 2, 6, 3, 5, 4):
+        if d:
+            arrived(fall.at[y, (z + NZ - d) % NZ], f1r.at[d])
+        for dy in (2, 1, 3):
+            f2_copy(d, dy).start()
+            drain.append(f2_copy(d, dy).wait_send)
 
     def f3_copy(y2):
         part = outv.at[pl.ds(pl.multiple_of(y2 * 128, 128), 128), half]
@@ -343,7 +345,8 @@
 
     for d in (0, 1, 3, 2):
         y2 = (y + d) % NY
-        arrived(fall.at[y2], f1r.at[y2])
+        if d:
+            arrived(fall.at[y2], f2r.at[y2])
         outv[pl.ds(pl.multiple_of(y2 * 128, 128), 128), half] = fall[y2].reshape(128, 128).T
         f3_copy(y2).start()
     drain += [f3_copy(y2).wait_send for y2 in range(NY)]
@@ -380,7 +383,7 @@
             vm((16, 128), F32), vm((16, 128), F32), vm((4, 8, 16, 128), F32),
             dma((6, 2)), dma, dma, dma((2,)), dma((2,)), dma((4,)), dma, dma((8,)), dma((4,)),
             dma((2, 4)), dma((2,)), dma((2, 8)), dma((2,)), dma((2, 4)), dma,
-            dma((4, 4)), dma((3,)), dma, dma, dma((4, 8)), dma((4,)), dma((4,)), dma,
+            dma((4, 4)), dma((3,)), dma, dma, dma((8,)), dma((8,)), dma((8, 4)), dma((4,)), dma((4,)), dma,
         ],
         compiler_params=pltpu.CompilerParams(collective_id=0, has_side_effects=True),
     )(live, targets, child_rhs, child_diag, child_off, top_rhs, top_factor.T, top_diag)

time: 61.8 us -> 61.7 us (level)
  no operation moved by 1% of the time
where the time goes in v4:
time: 61.7 us; the launch traced here: 61.6 us
  Pallas kernels  59.4 us (96%)
  local copies, waits for them, and re-layouts  1.59 us (3%)
  between operations  0.64 us (1%)
    pallas_call x1, Pallas kernels, shards(): pl.pallas_call(kernel, out_shape=(pltpu.VMEM(child_rhs.shape, F32), pltpu...  59.4 us
    unnamed x2, local copies, waits for them, and re-layouts  1.59 us

profile of v4, /device:TPU:7, one launch (start us, length us, event | category | flops | bytes accessed | tf_op | source)
XLA Modules:
  0.0 61.6 jit_solution(6900932411613496258)
XLA Ops:
  0.6 59.4 %shard_map.95 = (f32[2,256,256]{2,1,0:T(8,128)S(1)}, f32[512,256]{1,0:T(8,128)S(1)}) custom-call(s32[2]{0:T(128)} %live_ref.1, s32[2,256]{1,0:T(2,128)} %targ_ref.1, f32[2,256,256]{2,1,0:T(8,128)} %rhs_hbm.1, f32[2,256,256]{2,1,0:T(8,128)} %diag_hbm.1, f32[2,256,256]{2,1,0:T(8,128)} %off_hbm.1, f32[512,256]{1,0:T(8,128)} %trhs_hbm.1, f32[64,512]{1,0:T(8,128)} %bitcast.1, ...), custom_call_target="tpu_custom_call" | custom-call | tf_op jit(solution)/shard_map/pallas_call | solution.py:361
  60.0 0.8 %copy.12 = f32[2,256,256]{2,1,0:T(8,128)} copy(f32[2,256,256]{2,1,0:T(8,128)S(1)} %get-tuple-element.2) | data formatting | bytes 1048576
  60.8 0.8 %copy.13 = f32[512,256]{1,0:T(8,128)} copy(f32[512,256]{1,0:T(8,128)S(1)} %get-tuple-element.3) | data formatting | bytes 1048576

commit v5 on v4

--- a/solution.py
+++ b/solution.py
@@ -53,9 +53,11 @@
     live_ref, targ_ref, rhs_hbm, diag_hbm, off_hbm, trhs_hbm, fac_hbm, td_hbm,
     csol_v, outv,
     rhs_v, diag_v, off_v, tile_v, trhs_v, fac_v, td_v,
-    tg, trecv, tcol, tt, cbuf, s1recv, s2src, s2recv, s3src, s3recv,
+    tg, trecv, tcol, tt, cbuf, axrecv, ybuf, byrecv, ysum, bxrecv, azsrc, azrecv, bzsrc, bzrecv,
+    aysrc, ayrecv, cysrc, cyrecv, upd,
     rhst, tinv, gsrc, grecv, gparts, fsrc, xrecv, frecv, fown, fall,
-    load_sem, tgs, tgr, cs, cr, gas, gar, gs, gr, s1s, s1r, s2s, s2r, s3s, s3r, xs, xr, fps, fpr, f1s, f1r, f2s, f2r, f3s, f3r,
+    load_sem, tgs, tgr, cs, cr, gas, gar, gs, gr, axs, axr, bys, byr, bxs, bxr, azs, azr,
+    bzs, bzr, ays, ayr, cys, cyr, xs, xr, fps, fpr, f1s, f1r, f2s, f2r, f3s, f3r,
 ):
     leaf, x, col = lax.axis_index("leaf"), lax.axis_index("row"), lax.axis_index("col")
     y, z = col % NY, col // NY
@@ -147,30 +149,46 @@
         tt[128:256, 512 + 256 * s : 768 + 256 * s] = rest
     lane = lax.broadcasted_iota(jnp.int32, (1024, 128), 1)
 
-    def contrib(q, d):
-        block = (x + d) % NX
-        rel = tcol[...] - (block * 512 + q * 256).astype(F32)
+    def contrib(start):
+        rel = tcol[...] - start.astype(F32)
         lanes = lane.astype(F32)
         hot = jnp.concatenate(
             [jnp.where(rel == lanes, 1.0, 0.0), jnp.where(rel == lanes + 128.0, 1.0, 0.0)], axis=1
         ).astype(BF16)
         both = dot(tt[...], hot)
-        cbuf[q, d] = both[0:128] + both[128:256]
-
-    def s1_copy(q, d):
-        return remote(
-            cbuf.at[q, d], s1recv.at[q, d - 1], s1s.at[q, d], s1r.at[q], leaf, (x + d) % NX, y, z
-        )
-
-    for q in range(2):
-
-        def s1_step(d, _, q=q):
-            contrib(q, d)
-            s1_copy(q, d).start()
-            return 0
-
-        lax.fori_loop(1, NX, s1_step, 0)
-        drain += [s1_copy(q, d).wait_send for d in range(1, NX)]
+        return both[0:128] + both[128:256]
+
+    def ax_copy(d):
+        return remote(cbuf.at[d], axrecv.at[d - 1], axs.at[d], axr, leaf, (x + d) % NX, y, z)
+
+    def by_copy(d, b):
+        y2 = (y + d) % NY
+        return remote(ybuf.at[y2, b], byrecv.at[d - 1, b], bys.at[d, b], byr, leaf, x, y2, z)
+
+    def lower(d):
+        cbuf[d] = contrib((x + d) % NX * 512)
+
+    def upper(b, _):
+        value = contrib(b * 512 + 256)
+        for part in range(NY):
+            ybuf[part, b] = value[
+                part % 2 * 64 : part % 2 * 64 + 64, part // 2 * 128 : part // 2 * 128 + 128
+            ]
+        for d in (2, 1, 3):
+            by_copy(d, b).start()
+        return 0
+
+    def lower_upper(i, _):
+        d = (i * 2 + 1) % NX + i // 2
+        lower(d)
+        ax_copy(d).start()
+        upper(i, 0)
+        return 0
+
+    lax.fori_loop(0, 3, lower_upper, 0)
+    upper(jnp.int32(3), 0)
+    drain += [ax_copy(d).wait_send for d in range(1, NX)]
+    drain += [by_copy(d, b).wait_send for d in range(1, NY) for b in range(NX)]
 
     giver = (leaf == z % 2) & (z // 2 < x)
     for load in loads[6:]:
@@ -218,63 +236,109 @@
     tinv[0], tinv[1] = split((low + jnp.where(eye, 1.0, 0.0)).T)
     rhst[...] = trhs_v[pl.ds(col0, 256), :].T
 
-    for q in range(2):
-        contrib(q, 0)
-
-    def s2_copy(q, e):
+    lower(0)
+
+    arrived(byrecv, byr)
+
+    def bx_copy(d):
+        block = (x + d) % NX
+        return remote(ysum.at[block], bxrecv.at[d - 1], bxs.at[d], bxr, leaf, block, y, z)
+
+    def add_y(d):
+        b = (x + d) % NX
+        ysum[b] = ybuf[y, b] + byrecv[0, b] + byrecv[1, b] + byrecv[2, b]
+
+    for d in (2, 1, 3):
+        add_y(d)
+        bx_copy(d).start()
+        drain.append(bx_copy(d).wait_send)
+    add_y(0)
+
+    def az_copy(e):
         z2 = (z + e) % NZ
-        return remote(
-            s2src.at[q, z2], s2recv.at[q, e - 1], s2s.at[q, e], s2r.at[q], leaf, x, y, z2
-        )
-
-    for q in range(2):
-        arrived(s1recv.at[q], s1r.at[q])
-        s2src[q] = (cbuf[q, 0] + s1recv[q, 0] + s1recv[q, 1] + s1recv[q, 2]).reshape(NZ, 16, 256)
-
-        def s2_step(e, _, q=q):
-            s2_copy(q, e).start()
-            return 0
-
-        lax.fori_loop(1, NZ, s2_step, 0)
-        drain += [s2_copy(q, e).wait_send for e in range(1, NZ)]
+        return remote(azsrc.at[z2], azrecv.at[e - 1], azs.at[e], azr, leaf, x, y, z2)
+
+    arrived(axrecv, axr)
+    azsrc[...] = (cbuf[0] + axrecv[0] + axrecv[1] + axrecv[2]).reshape(NZ, 16, 256)
+    for e in (4, 3, 5, 2, 6, 1, 7):
+        az_copy(e).start()
+        drain.append(az_copy(e).wait_send)
+
+    keeper = z // 4 == y % 2
+
+    def bz_copy(i):
+        z2 = y % 2 * 4 + i
+        return z2 != z, remote(bzsrc.at[i], bzrecv.at[z], bzs.at[i], bzr, leaf, x, y, z2)
+
+    arrived(bxrecv, bxr)
+    bzsrc[...] = (ysum[x] + bxrecv[0] + bxrecv[1] + bxrecv[2]).reshape(4, 16, 128)
+    for i in range(4):
+        away, copy = bz_copy(i)
+        pl.when(away)(copy.start)
+
+    def bz_drain():
+        for i in range(4):
+            away, copy = bz_copy(i)
+            pl.when(away)(copy.wait_send)
+
+    drain.append(bz_drain)
+    pl.when(keeper)(local(bzsrc.at[z % 4], bzrecv.at[z], bzr).start)
     g_forward()
 
-    def s3_copy(q, dy):
-        y2 = (y + dy) % NY
-        return remote(s3src.at[q], s3recv.at[leaf, dy], s3s.at[q, dy], s3r, q, x, y2, z)
-
-    for q in range(2):
-        arrived(s2recv.at[q], s2r.at[q])
-        total = s2src[q, z]
-        for e in range(NZ - 1):
-            total = total + s2recv[q, e]
-        s3src[q] = total
-        for dy in range(1, NY):
-            s3_copy(q, dy).start()
-
-        @pl.when(leaf == q)
-        def _(q=q):
-            local(s3src.at[q], s3recv.at[leaf, 0], s3r).start()
-
-        @pl.when(leaf != q)
-        def _(q=q):
-            s3_copy(q, 0).start()
-
-        def s3_drain(q=q):
+    def ay_copy(dy):
+        return remote(aysrc, ayrecv.at[leaf, dy], ays.at[dy], ayr, 0, x, (y + dy) % NY, z)
+
+    arrived(azrecv, azr)
+    total = azsrc[z]
+    for e in range(NZ - 1):
+        total = total + azrecv[e]
+    aysrc[...] = total
+    for dy in (2, 1, 3):
+        ay_copy(dy).start()
+        drain.append(ay_copy(dy).wait_send)
+    pl.when(leaf == 0)(local(aysrc, ayrecv.at[leaf, 0], ayr).start)
+    pl.when(leaf == 1)(ay_copy(0).start)
+    drain.append(lambda: pl.when(leaf == 1)(ay_copy(0).wait_send))
+
+    def cy_copy(dy):
+        return remote(cysrc, cyrecv.at[leaf, y // 2], cys.at[dy], cyr, 1, x, (y + dy) % NY, z)
+
+    @pl.when(keeper)
+    def _():
+        arrived(bzrecv, bzr)
+        total = bzrecv[0]
+        for e in range(1, NZ):
+            total = total + bzrecv[e]
+        cysrc[...] = total
+        for dy in (2, 1, 3):
+            cy_copy(dy).start()
+        pl.when(leaf == 1)(local(cysrc, cyrecv.at[leaf, y // 2], cyr).start)
+        pl.when(leaf == 0)(cy_copy(0).start)
+
+    def cy_drain():
+        @pl.when(keeper)
+        def _():
             for dy in range(1, NY):
-                s3_copy(q, dy).wait_send()
-
-            @pl.when(leaf != q)
-            def _():
-                s3_copy(q, 0).wait_send()
-
-        drain.append(s3_drain)
-
-    arrived(s3recv, s3r)
+                cy_copy(dy).wait_send()
+            pl.when(leaf == 0)(cy_copy(0).wait_send)
+
+    drain.append(cy_drain)
+
+    @pl.when(leaf == 0)
+    def _():
+        arrived(ayrecv, ayr)
+        for h in range(2):
+            upd[h] = ayrecv[h, 0] + ayrecv[h, 1] + ayrecv[h, 2] + ayrecv[h, 3]
+
+    @pl.when(leaf == 1)
+    def _():
+        arrived(cyrecv, cyr)
+        for h in range(2):
+            upd[h] = jnp.concatenate([cyrecv[h, 0], cyrecv[h, 1]], axis=1)
+
     reds = []
     for h in range(2):
-        upd = s3recv[h, 0] + s3recv[h, 1] + s3recv[h, 2] + s3recv[h, 3]
-        reds.append(rhst[pl.ds(pl.multiple_of(h * 128 + z * 16, 16), 16), :] - upd)
+        reds.append(rhst[pl.ds(pl.multiple_of(h * 128 + z * 16, 16), 16), :] - upd[h])
     acc = dot3p(jnp.concatenate(reds, axis=0), tinv[0], tinv[1])
     fsrc[...] = acc.reshape(2, 16, 128)
 
@@ -374,15 +438,18 @@
             vm((2, 256, 256), F32),
             vm((512, 256), F32), vm((64, 512), F32), vm((512, 512), F32),
             vm((2, 2, 8, 256), F32), vm((2, 256, 128), F32), vm((1024, 128), F32), vm((256, 1024), BF16),
-            vm((2, 4, 128, 256), F32), vm((2, 3, 128, 256), F32),
-            vm((2, 8, 16, 256), F32), vm((2, 7, 16, 256), F32),
-            vm((2, 16, 256), F32), vm((2, 4, 16, 256), F32),
+            vm((4, 128, 256), F32), vm((3, 128, 256), F32),
+            vm((4, 4, 64, 128), F32), vm((3, 4, 64, 128), F32), vm((4, 64, 128), F32), vm((3, 64, 128), F32),
+            vm((8, 16, 256), F32), vm((7, 16, 256), F32), vm((4, 16, 128), F32), vm((8, 16, 128), F32),
+            vm((16, 256), F32), vm((2, 4, 16, 256), F32), vm((16, 128), F32), vm((2, 2, 16, 128), F32),
+            vm((2, 16, 256), F32),
             vm((256, 256), F32), vm((2, 256, 128), BF16),
             vm((4, 64, 128), F32), vm((3, 4, 64, 128), F32), vm((3, 2, 256, 128), BF16),
             vm((2, 16, 128), F32), vm((3, 2, 2, 2, 16, 128), F32),
             vm((16, 128), F32), vm((16, 128), F32), vm((4, 8, 16, 128), F32),
             dma((6, 2)), dma, dma, dma((2,)), dma((2,)), dma((4,)), dma, dma((8,)), dma((4,)),
-            dma((2, 4)), dma((2,)), dma((2, 8)), dma((2,)), dma((2, 4)), dma,
+            dma((4,)), dma, dma((4, 4)), dma, dma((4,)), dma, dma((8,)), dma,
+            dma((4,)), dma, dma((4,)), dma, dma((4,)), dma,
             dma((4, 4)), dma((3,)), dma, dma, dma((8,)), dma((8,)), dma((8, 4)), dma((4,)), dma((4,)), dma,
         ],
         compiler_params=pltpu.CompilerParams(collective_id=0, has_side_effects=True),

time: 61.7 us -> 58.6 us (0.950)
  Pallas kernels: 59.4 us -> 56.2 us
    pallas_call x1, Pallas kernels: 59.4 us -> 56.2 us  [shards(): pl.pallas_call(kernel, out_shape=(pltpu.VMEM(child_rhs.shape, F32), pltpu...]
where the time goes in v5:
time: 58.6 us; the launch traced here: 58.5 us
  Pallas kernels  56.2 us (96%)
  local copies, waits for them, and re-layouts  1.59 us (3%)
  between operations  0.64 us (1%)
    pallas_call x1, Pallas kernels, shards(): pl.pallas_call(kernel, out_shape=(pltpu.VMEM(child_rhs.shape, F32), pltpu...  56.2 us
    unnamed x2, local copies, waits for them, and re-layouts  1.59 us

profile of v5, /device:TPU:7, one launch (start us, length us, event | category | flops | bytes accessed | tf_op | source)
XLA Modules:
  0.0 58.5 jit_solution(12892746810130674176)
XLA Ops:
  0.6 56.2 %shard_map.95 = (f32[2,256,256]{2,1,0:T(8,128)S(1)}, f32[512,256]{1,0:T(8,128)S(1)}) custom-call(s32[2]{0:T(128)} %live_ref.1, s32[2,256]{1,0:T(2,128)} %targ_ref.1, f32[2,256,256]{2,1,0:T(8,128)} %rhs_hbm.1, f32[2,256,256]{2,1,0:T(8,128)} %diag_hbm.1, f32[2,256,256]{2,1,0:T(8,128)} %off_hbm.1, f32[512,256]{1,0:T(8,128)} %trhs_hbm.1, f32[64,512]{1,0:T(8,128)} %bitcast.1, ...), custom_call_target="tpu_custom_call" | custom-call | tf_op jit(solution)/shard_map/pallas_call | solution.py:425
  56.9 0.8 %copy.12 = f32[2,256,256]{2,1,0:T(8,128)} copy(f32[2,256,256]{2,1,0:T(8,128)S(1)} %get-tuple-element.2) | data formatting | bytes 1048576
  57.7 0.8 %copy.13 = f32[512,256]{1,0:T(8,128)} copy(f32[512,256]{1,0:T(8,128)S(1)} %get-tuple-element.3) | data formatting | bytes 1048576

commit v6 on v5

--- a/solution.py
+++ b/solution.py
@@ -418,11 +418,25 @@
     finish()
 
 
+def write_out(csol_v, top_v, csol_hbm, top_hbm, sem):
+    copies = [pltpu.make_async_copy(csol_v.at[s], csol_hbm.at[s], sem.at[s]) for s in range(2)]
+    copies += [
+        pltpu.make_async_copy(
+            top_v.at[256 * s : 256 * s + 256], top_hbm.at[256 * s : 256 * s + 256], sem.at[2 + s]
+        )
+        for s in range(2)
+    ]
+    for copy in copies:
+        copy.start()
+    for copy in copies:
+        copy.wait()
+
+
 def shards(child_rhs, child_diag, child_off, live, targets, top_rhs, top_factor, top_diag):
     any_ = pl.BlockSpec(memory_space=pl.ANY)
     vm = pltpu.VMEM
     dma = pltpu.SemaphoreType.DMA
-    return pl.pallas_call(
+    solved = pl.pallas_call(
         kernel,
         out_shape=(
             pltpu.VMEM(child_rhs.shape, F32),
@@ -454,6 +468,13 @@
         ],
         compiler_params=pltpu.CompilerParams(collective_id=0, has_side_effects=True),
     )(live, targets, child_rhs, child_diag, child_off, top_rhs, top_factor.T, top_diag)
+    return pl.pallas_call(
+        write_out,
+        out_shape=tuple(jax.ShapeDtypeStruct(a.shape, F32) for a in (child_rhs, top_rhs)),
+        in_specs=[pl.BlockSpec(memory_space=pltpu.VMEM)] * 2,
+        out_specs=(any_, any_),
+        scratch_shapes=[dma((4,))],
+    )(*(pltpu.with_memory_space_constraint(a, pltpu.VMEM) for a in solved))
 
 
 def solution(mesh):

time: 58.6 us -> 58 us (0.990)
  local copies, waits for them, and re-layouts: 1.59 us -> 0 us
  Pallas kernels: 56.2 us -> 57.2 us
    unnamed x2 -> x0, local copies, waits for them, and re-layouts: 1.59 us -> none
    pallas_call x0 -> x1, Pallas kernels: none -> 1 us  [shards(): pl.pallas_call(write_out, out_shape=tuple((jax.ShapeDtypeStruct(a.shape,...]
where the time goes in v6:
time: 58 us; the launch traced here: 57.9 us
  Pallas kernels  57.2 us (99%)
  between operations  0.64 us (1%)
    pallas_call x1, Pallas kernels, shards(): pl.pallas_call(kernel, out_shape=(pltpu.VMEM(child_rhs.shape, F32), pltpu...  56.2 us

profile of v6, /device:TPU:7, one launch (start us, length us, event | category | flops | bytes accessed | tf_op | source)
XLA Modules:
  0.0 57.9 jit_solution(1254068478870674708)
XLA Ops:
  0.6 56.2 %shard_map.95 = (f32[2,256,256]{2,1,0:T(8,128)S(1)}, f32[512,256]{1,0:T(8,128)S(1)}) custom-call(s32[2]{0:T(128)} %live_ref.1, s32[2,256]{1,0:T(2,128)} %targ_ref.1, f32[2,256,256]{2,1,0:T(8,128)} %rhs_hbm.1, f32[2,256,256]{2,1,0:T(8,128)} %diag_hbm.1, f32[2,256,256]{2,1,0:T(8,128)} %off_hbm.1, f32[512,256]{1,0:T(8,128)} %trhs_hbm.1, f32[64,512]{1,0:T(8,128)} %bitcast.1, ...), custom_call_target="tpu_custom_call" | custom-call | tf_op jit(solution)/shard_map/pallas_call | solution.py:439
  56.9 1.0 %shard_map.96 = (f32[2,256,256]{2,1,0:T(8,128)}, f32[512,256]{1,0:T(8,128)}) custom-call(f32[2,256,256]{2,1,0:T(8,128)S(1)} %get-tuple-element.4.csol_v, f32[512,256]{1,0:T(8,128)S(1)} %get-tuple-element.5.top_v), custom_call_target="tpu_custom_call" | custom-call | tf_op jit(solution)/shard_map/pallas_call | solution.py:471

commit v7 on v6

--- a/solution.py
+++ b/solution.py
@@ -56,7 +56,7 @@
     tg, trecv, tcol, tt, cbuf, axrecv, ybuf, byrecv, ysum, bxrecv, azsrc, azrecv, bzsrc, bzrecv,
     aysrc, ayrecv, cysrc, cyrecv, upd,
     rhst, tinv, gsrc, grecv, gparts, fsrc, xrecv, frecv, fown, fall,
-    load_sem, tgs, tgr, cs, cr, gas, gar, gs, gr, axs, axr, bys, byr, bxs, bxr, azs, azr,
+    near, load_sem, tgs, tgr, cs, cr, gas, gar, gs, gr, axs, axr, bys, byr, bxs, bxr, azs, azr,
     bzs, bzr, ays, ayr, cys, cyr, xs, xr, fps, fpr, f1s, f1r, f2s, f2r, f3s, f3r,
 ):
     leaf, x, col = lax.axis_index("leaf"), lax.axis_index("row"), lax.axis_index("col")
@@ -103,7 +103,7 @@
         greet(leaf, (x + d) % NX, y, z)
     for d in range(1, NY):
         greet(leaf, x, (y + d) % NY, z)
-    for d in range(1, NZ):
+    for d in (1, NZ - 1):
         greet(leaf, x, y, (z + d) % NZ)
 
     lane = lax.broadcasted_iota(jnp.int32, (1, 256), 1)
@@ -120,7 +120,15 @@
         loads[3 * s + 2].wait()
         tile_v[s] = dot3(off_v[s], sol)
 
-    pl.semaphore_wait(barrier, 1 + NX - 1 + NY - 1 + NZ - 1)
+    pl.semaphore_wait(barrier, 1 + NX - 1 + NY - 1 + 2)
+
+    def spread(step):
+        for d in (step, NZ - step):
+            pl.semaphore_signal(
+                near.at[step - 1], inc=1, device_id=(leaf, x, (z + d) % NZ * NY + y), device_id_type=MESH
+            )
+
+    spread(1)
     tg_copy = remote(tg.at[0], tg.at[1], tgs, tgr, sibling, x, y, z)
     tg_copy.start()
     drain.append(tg_copy.wait_send)
@@ -187,6 +195,8 @@
 
     lax.fori_loop(0, 3, lower_upper, 0)
     upper(jnp.int32(3), 0)
+    pl.semaphore_wait(near.at[0], 2)
+    spread(2)
     drain += [ax_copy(d).wait_send for d in range(1, NX)]
     drain += [by_copy(d, b).wait_send for d in range(1, NY) for b in range(NX)]
 
@@ -237,6 +247,7 @@
     rhst[...] = trhs_v[pl.ds(col0, 256), :].T
 
     lower(0)
+    pl.semaphore_wait(near.at[1], 2)
 
     arrived(byrecv, byr)
 
@@ -461,6 +472,7 @@
             vm((4, 64, 128), F32), vm((3, 4, 64, 128), F32), vm((3, 2, 256, 128), BF16),
             vm((2, 16, 128), F32), vm((3, 2, 2, 2, 16, 128), F32),
             vm((16, 128), F32), vm((16, 128), F32), vm((4, 8, 16, 128), F32),
+            pltpu.SemaphoreType.REGULAR((2,)),
             dma((6, 2)), dma, dma, dma((2,)), dma((2,)), dma((4,)), dma, dma((8,)), dma((4,)),
             dma((4,)), dma, dma((4, 4)), dma, dma((4,)), dma, dma((8,)), dma,
             dma((4,)), dma, dma((4,)), dma, dma((4,)), dma,

time: 58 us -> 56.4 us (0.972)
  Pallas kernels: 57.2 us -> 55.6 us
    pallas_call x1, Pallas kernels: 56.2 us -> 54.6 us  [shards(): pl.pallas_call(kernel, out_shape=(pltpu.VMEM(child_rhs.shape, F32), pltpu...]
where the time goes in v7:
time: 56.4 us; the launch traced here: 56.3 us
  Pallas kernels  55.6 us (99%)
  between operations  0.64 us (1%)
    pallas_call x1, Pallas kernels, shards(): pl.pallas_call(kernel, out_shape=(pltpu.VMEM(child_rhs.shape, F32), pltpu...  54.6 us

profile of v7, /device:TPU:7, one launch (start us, length us, event | category | flops | bytes accessed | tf_op | source)
XLA Modules:
  0.0 56.3 jit_solution(15003326573245378060)
XLA Ops:
  0.6 54.6 %shard_map.95 = (f32[2,256,256]{2,1,0:T(8,128)S(1)}, f32[512,256]{1,0:T(8,128)S(1)}) custom-call(s32[2]{0:T(128)} %live_ref.1, s32[2,256]{1,0:T(2,128)} %targ_ref.1, f32[2,256,256]{2,1,0:T(8,128)} %rhs_hbm.1, f32[2,256,256]{2,1,0:T(8,128)} %diag_hbm.1, f32[2,256,256]{2,1,0:T(8,128)} %off_hbm.1, f32[512,256]{1,0:T(8,128)} %trhs_hbm.1, f32[64,512]{1,0:T(8,128)} %bitcast.1, ...), custom_call_target="tpu_custom_call" | custom-call | tf_op jit(solution)/shard_map/pallas_call | solution.py:450
  55.3 1.0 %shard_map.96 = (f32[2,256,256]{2,1,0:T(8,128)}, f32[512,256]{1,0:T(8,128)}) custom-call(f32[2,256,256]{2,1,0:T(8,128)S(1)} %get-tuple-element.4.csol_v, f32[512,256]{1,0:T(8,128)S(1)} %get-tuple-element.5.top_v), custom_call_target="tpu_custom_call" | custom-call | tf_op jit(solution)/shard_map/pallas_call | solution.py:483

commit v8 on v7

--- a/solution.py
+++ b/solution.py
@@ -396,6 +396,8 @@
     pair.wait_recv()
     fown[...] = fsrc[leaf] + frecv[...]
 
+    late = []
+
     def f1_copy(d):
         return remote(fown, fall.at[y, z], f1s.at[d], f1r.at[d], leaf, x, y, (z + d) % NZ)
 
@@ -405,14 +407,16 @@
 
     for d in (4, 3, 5, 2, 6, 1, 7):
         f1_copy(d).start()
-        drain.append(f1_copy(d).wait_send)
+        late.append(f1_copy(d).wait_send)
     fall[y, z] = fown[...]
     for d in (0, 1, 7, 2, 6, 3, 5, 4):
         if d:
             arrived(fall.at[y, (z + NZ - d) % NZ], f1r.at[d])
         for dy in (2, 1, 3):
             f2_copy(d, dy).start()
-            drain.append(f2_copy(d, dy).wait_send)
+            late.append(f2_copy(d, dy).wait_send)
+        if d == 0:
+            finish()
 
     def f3_copy(y2):
         part = outv.at[pl.ds(pl.multiple_of(y2 * 128, 128), 128), half]
@@ -424,9 +428,11 @@
             arrived(fall.at[y2], f2r.at[y2])
         outv[pl.ds(pl.multiple_of(y2 * 128, 128), 128), half] = fall[y2].reshape(128, 128).T
         f3_copy(y2).start()
-    drain += [f3_copy(y2).wait_send for y2 in range(NY)]
+    for wait in late:
+        wait()
     arrived(outv.at[:, pl.ds(pl.multiple_of(sibling * 128, 128), 128)], f3r)
-    finish()
+    for y2 in range(NY):
+        f3_copy(y2).wait_send()
 
 
 def write_out(csol_v, top_v, csol_hbm, top_hbm, sem):

time: 56.4 us -> 56.3 us (level)
  no operation moved by 1% of the time
where the time goes in v8:
time: 56.3 us; the launch traced here: 56.1 us
  Pallas kernels  55.5 us (99%)
  between operations  0.64 us (1%)
    pallas_call x1, Pallas kernels, shards(): pl.pallas_call(kernel, out_shape=(pltpu.VMEM(child_rhs.shape, F32), pltpu...  54.5 us

profile of v8, /device:TPU:7, one launch (start us, length us, event | category | flops | bytes accessed | tf_op | source)
XLA Modules:
  0.0 56.1 jit_solution(18386258223604966974)
XLA Ops:
  0.6 54.5 %shard_map.95 = (f32[2,256,256]{2,1,0:T(8,128)S(1)}, f32[512,256]{1,0:T(8,128)S(1)}) custom-call(s32[2]{0:T(128)} %live_ref.1, s32[2,256]{1,0:T(2,128)} %targ_ref.1, f32[2,256,256]{2,1,0:T(8,128)} %rhs_hbm.1, f32[2,256,256]{2,1,0:T(8,128)} %diag_hbm.1, f32[2,256,256]{2,1,0:T(8,128)} %off_hbm.1, f32[512,256]{1,0:T(8,128)} %trhs_hbm.1, f32[64,512]{1,0:T(8,128)} %bitcast.1, ...), custom_call_target="tpu_custom_call" | custom-call | tf_op jit(solution)/shard_map/pallas_call | solution.py:456
  55.1 1.0 %shard_map.96 = (f32[2,256,256]{2,1,0:T(8,128)}, f32[512,256]{1,0:T(8,128)}) custom-call(f32[2,256,256]{2,1,0:T(8,128)S(1)} %get-tuple-element.4.csol_v, f32[512,256]{1,0:T(8,128)S(1)} %get-tuple-element.5.top_v), custom_call_target="tpu_custom_call" | custom-call | tf_op jit(solution)/shard_map/pallas_call | solution.py:489

commit v9 on v8

--- a/solution.py
+++ b/solution.py
@@ -55,9 +55,9 @@
     rhs_v, diag_v, off_v, tile_v, trhs_v, fac_v, td_v,
     tg, trecv, tcol, tt, cbuf, axrecv, ybuf, byrecv, ysum, bxrecv, azsrc, azrecv, bzsrc, bzrecv,
     aysrc, ayrecv, cysrc, cyrecv, upd,
-    rhst, tinv, gsrc, grecv, gparts, fsrc, xrecv, frecv, fown, fall,
+    rhst, tinv, gsrc, grecv, gparts, gsib, lastrecv, fsrc, xrecv, frecv, fown, fall,
     near, load_sem, tgs, tgr, cs, cr, gas, gar, gs, gr, axs, axr, bys, byr, bxs, bxr, azs, azr,
-    bzs, bzr, ays, ayr, cys, cyr, xs, xr, fps, fpr, f1s, f1r, f2s, f2r, f3s, f3r,
+    bzs, bzr, ays, ayr, cys, cyr, lasts, lastr, ess, esr, xs, xr, fps, fpr, f1s, f1r, f2s, f2r, f3s, f3r,
 ):
     leaf, x, col = lax.axis_index("leaf"), lax.axis_index("row"), lax.axis_index("col")
     y, z = col % NY, col // NY
@@ -358,7 +358,7 @@
             fsrc, xrecv.at[k, leaf, y % 2], xs.at[x2, y2], xr.at[k], y // 2, x2, y2, z
         )
 
-    for k in range(NX - 1):
+    for k in range(NX - 2):
 
         @pl.when(x == k)
         def _(k=k):
@@ -390,11 +390,56 @@
 
         drain.append(x_drain)
 
+    def last_copy(h, y2):
+        return remote(fsrc.at[h], lastrecv.at[leaf, y], lasts.at[h, y2], lastr, h, NX - 1, y2, z)
+
+    other_g = remote(grecv.at[NX - 2], gsib, ess, esr, sibling, x, y, z)
     pair = remote(fsrc.at[sibling], frecv, fps, fpr, sibling, x, y, z)
+
+    @pl.when(x == NX - 2)
+    def _():
+        for y2 in range(NY):
+            for h in range(2):
+                last_copy(h, y2).start()
+
     pair.start()
     drain.append(pair.wait_send)
+
+    @pl.when(x == NX - 1)
+    def _():
+        @pl.when(z != 2 * (NX - 2) + leaf)
+        def _():
+            arrived(grecv.at[NX - 2], gr.at[NX - 2])
+
+        other_g.start()
+
     pair.wait_recv()
     fown[...] = fsrc[leaf] + frecv[...]
+
+    @pl.when(x == NX - 1)
+    def _():
+        own = split(grecv[NX - 2].reshape(256, 128))
+        other_g.wait_recv()
+        other = split(gsib[...].reshape(256, 128))
+        arrived(lastrecv, lastr)
+
+        def solved(core):
+            first = lastrecv[0, 2 * core] + lastrecv[1, 2 * core]
+            second = lastrecv[0, 2 * core + 1] + lastrecv[1, 2 * core + 1]
+            return jnp.concatenate([first, second], axis=1)
+
+        fown[...] = fown[...] - (dot3p(solved(leaf), *own) + dot3p(solved(sibling), *other))
+
+    def last_drain():
+        @pl.when(x == NX - 2)
+        def _():
+            for y2 in range(NY):
+                for h in range(2):
+                    last_copy(h, y2).wait_send()
+
+        pl.when(x == NX - 1)(other_g.wait_send)
+
+    drain.append(last_drain)
 
     late = []
 
@@ -476,12 +521,14 @@
             vm((2, 16, 256), F32),
             vm((256, 256), F32), vm((2, 256, 128), BF16),
             vm((4, 64, 128), F32), vm((3, 4, 64, 128), F32), vm((3, 2, 256, 128), BF16),
+            vm((4, 64, 128), F32), vm((2, 4, 16, 128), F32),
             vm((2, 16, 128), F32), vm((3, 2, 2, 2, 16, 128), F32),
             vm((16, 128), F32), vm((16, 128), F32), vm((4, 8, 16, 128), F32),
             pltpu.SemaphoreType.REGULAR((2,)),
             dma((6, 2)), dma, dma, dma((2,)), dma((2,)), dma((4,)), dma, dma((8,)), dma((4,)),
             dma((4,)), dma, dma((4, 4)), dma, dma((4,)), dma, dma((8,)), dma,
             dma((4,)), dma, dma((4,)), dma, dma((4,)), dma,
+            dma((2, 4)), dma, dma, dma,
             dma((4, 4)), dma((3,)), dma, dma, dma((8,)), dma((8,)), dma((8, 4)), dma((4,)), dma((4,)), dma,
         ],
         compiler_params=pltpu.CompilerParams(collective_id=0, has_side_effects=True),

time: 56.3 us -> 55.7 us (0.989)
  no operation moved by 1% of the time
where the time goes in v9:
time: 55.7 us; the launch traced here: 55.6 us
  Pallas kernels  55 us (99%)
  between operations  0.64 us (1%)
    pallas_call x1, Pallas kernels, shards(): pl.pallas_call(kernel, out_shape=(pltpu.VMEM(child_rhs.shape, F32), pltpu...  54 us

profile of v9, /device:TPU:7, one launch (start us, length us, event | category | flops | bytes accessed | tf_op | source)
XLA Modules:
  0.0 55.6 jit_solution(3348814627505827119)
XLA Ops:
  0.6 54.0 %shard_map.95 = (f32[2,256,256]{2,1,0:T(8,128)S(1)}, f32[512,256]{1,0:T(8,128)S(1)}) custom-call(s32[2]{0:T(128)} %live_ref.1, s32[2,256]{1,0:T(2,128)} %targ_ref.1, f32[2,256,256]{2,1,0:T(8,128)} %rhs_hbm.1, f32[2,256,256]{2,1,0:T(8,128)} %diag_hbm.1, f32[2,256,256]{2,1,0:T(8,128)} %off_hbm.1, f32[512,256]{1,0:T(8,128)} %trhs_hbm.1, f32[64,512]{1,0:T(8,128)} %bitcast.1, ...), custom_call_target="tpu_custom_call" | custom-call | tf_op jit(solution)/shard_map/pallas_call | solution.py:501
  54.6 1.0 %shard_map.96 = (f32[2,256,256]{2,1,0:T(8,128)}, f32[512,256]{1,0:T(8,128)}) custom-call(f32[2,256,256]{2,1,0:T(8,128)S(1)} %get-tuple-element.4.csol_v, f32[512,256]{1,0:T(8,128)S(1)} %get-tuple-element.5.top_v), custom_call_target="tpu_custom_call" | custom-call | tf_op jit(solution)/shard_map/pallas_call | solution.py:536

commit v10 on v9

--- a/solution.py
+++ b/solution.py
@@ -353,9 +353,9 @@
     acc = dot3p(jnp.concatenate(reds, axis=0), tinv[0], tinv[1])
     fsrc[...] = acc.reshape(2, 16, 128)
 
-    def x_copy(k, x2, y2):
+    def x_copy(k, x2, dy):
         return remote(
-            fsrc, xrecv.at[k, leaf, y % 2], xs.at[x2, y2], xr.at[k], y // 2, x2, y2, z
+            fsrc, xrecv.at[k, leaf, y % 2], xs.at[x2, dy], xr.at[k], y // 2, x2, (y + dy) % NY, z
         )
 
     for k in range(NX - 2):
@@ -363,8 +363,8 @@
         @pl.when(x == k)
         def _(k=k):
             for x2 in range(k + 1, NX):
-                for y2 in range(NY):
-                    x_copy(k, x2, y2).start()
+                for dy in (2, 1, 3, 0):
+                    x_copy(k, x2, dy).start()
 
         @pl.when(x > k)
         def _(k=k):
@@ -390,17 +390,19 @@
 
         drain.append(x_drain)
 
-    def last_copy(h, y2):
-        return remote(fsrc.at[h], lastrecv.at[leaf, y], lasts.at[h, y2], lastr, h, NX - 1, y2, z)
+    def last_copy(h, dy):
+        return remote(
+            fsrc.at[h], lastrecv.at[leaf, y], lasts.at[h, dy], lastr, h, NX - 1, (y + dy) % NY, z
+        )
 
     other_g = remote(grecv.at[NX - 2], gsib, ess, esr, sibling, x, y, z)
     pair = remote(fsrc.at[sibling], frecv, fps, fpr, sibling, x, y, z)
 
     @pl.when(x == NX - 2)
     def _():
-        for y2 in range(NY):
+        for dy in (2, 1, 3, 0):
             for h in range(2):
-                last_copy(h, y2).start()
+                last_copy(h, dy).start()
 
     pair.start()
     drain.append(pair.wait_send)

time: 55.7 us -> 55.3 us (level)
  no operation moved by 1% of the time
where the time goes in v10:
time: 55.3 us; the launch traced here: 55.1 us
  Pallas kernels  54.5 us (99%)
  between operations  0.64 us (1%)
    pallas_call x1, Pallas kernels, shards(): pl.pallas_call(kernel, out_shape=(pltpu.VMEM(child_rhs.shape, F32), pltpu...  53.5 us

profile of v10, /device:TPU:7, one launch (start us, length us, event | category | flops | bytes accessed | tf_op | source)
XLA Modules:
  0.0 55.1 jit_solution(16084726882704207173)
XLA Ops:
  0.6 53.5 %shard_map.95 = (f32[2,256,256]{2,1,0:T(8,128)S(1)}, f32[512,256]{1,0:T(8,128)S(1)}) custom-call(s32[2]{0:T(128)} %live_ref.1, s32[2,256]{1,0:T(2,128)} %targ_ref.1, f32[2,256,256]{2,1,0:T(8,128)} %rhs_hbm.1, f32[2,256,256]{2,1,0:T(8,128)} %diag_hbm.1, f32[2,256,256]{2,1,0:T(8,128)} %off_hbm.1, f32[512,256]{1,0:T(8,128)} %trhs_hbm.1, f32[64,512]{1,0:T(8,128)} %bitcast.1, ...), custom_call_target="tpu_custom_call" | custom-call | tf_op jit(solution)/shard_map/pallas_call | solution.py:503
  54.2 1.0 %shard_map.96 = (f32[2,256,256]{2,1,0:T(8,128)}, f32[512,256]{1,0:T(8,128)}) custom-call(f32[2,256,256]{2,1,0:T(8,128)S(1)} %get-tuple-element.4.csol_v, f32[512,256]{1,0:T(8,128)S(1)} %get-tuple-element.5.top_v), custom_call_target="tpu_custom_call" | custom-call | tf_op jit(solution)/shard_map/pallas_call | solution.py:538

commit v11 on v10

--- a/solution.py
+++ b/solution.py
@@ -277,13 +277,14 @@
 
     keeper = z // 4 == y % 2
 
-    def bz_copy(i):
+    def bz_copy(turn):
+        i = (z + turn) % 4
         z2 = y % 2 * 4 + i
         return z2 != z, remote(bzsrc.at[i], bzrecv.at[z], bzs.at[i], bzr, leaf, x, y, z2)
 
     arrived(bxrecv, bxr)
     bzsrc[...] = (ysum[x] + bxrecv[0] + bxrecv[1] + bxrecv[2]).reshape(4, 16, 128)
-    for i in range(4):
+    for i in (0, 1, 3, 2):
         away, copy = bz_copy(i)
         pl.when(away)(copy.start)
 

time: 55.3 us -> 55.2 us (level)
  no operation moved by 1% of the time
where the time goes in v11:
time: 55.2 us; the launch traced here: 55 us
  Pallas kernels  54.4 us (99%)
  between operations  0.64 us (1%)
    pallas_call x1, Pallas kernels, shards(): pl.pallas_call(kernel, out_shape=(pltpu.VMEM(child_rhs.shape, F32), pltpu...  53.4 us

profile of v11, /device:TPU:7, one launch (start us, length us, event | category | flops | bytes accessed | tf_op | source)
XLA Modules:
  0.0 55.0 jit_solution(7813910819723137378)
XLA Ops:
  0.6 53.4 %shard_map.95 = (f32[2,256,256]{2,1,0:T(8,128)S(1)}, f32[512,256]{1,0:T(8,128)S(1)}) custom-call(s32[2]{0:T(128)} %live_ref.1, s32[2,256]{1,0:T(2,128)} %targ_ref.1, f32[2,256,256]{2,1,0:T(8,128)} %rhs_hbm.1, f32[2,256,256]{2,1,0:T(8,128)} %diag_hbm.1, f32[2,256,256]{2,1,0:T(8,128)} %off_hbm.1, f32[512,256]{1,0:T(8,128)} %trhs_hbm.1, f32[64,512]{1,0:T(8,128)} %bitcast.1, ...), custom_call_target="tpu_custom_call" | custom-call | tf_op jit(solution)/shard_map/pallas_call | solution.py:504
  54.0 1.0 %shard_map.96 = (f32[2,256,256]{2,1,0:T(8,128)}, f32[512,256]{1,0:T(8,128)}) custom-call(f32[2,256,256]{2,1,0:T(8,128)S(1)} %get-tuple-element.4.csol_v, f32[512,256]{1,0:T(8,128)S(1)} %get-tuple-element.5.top_v), custom_call_target="tpu_custom_call" | custom-call | tf_op jit(solution)/shard_map/pallas_call | solution.py:539
